TPU v7x, 32 devices: a whole 2x2x4 slice. The times are simulated.
32 devices in a mesh: group: 2 (over x), tm: 16 (over z, y, core).
Axes of the slice: x: 2, y: 2, z: 4, core: 2. Of those that a mesh axis runs over, the one named last changes fastest.
Arguments:
- records: float32 [256, 262144], P('group', 'tm'), parts along dimension 0, may hold values from -6 to 6
- labels: int32 [256], P('group'), parts along dimension 0, may hold values from 0 to 1
- first_weight: bfloat16 [131072, 1024], P('tm'), may hold values from -0.015625 to 0.015625
- first_bias: float32 [1024], replicated, may hold values from -3 to 3
- second_weight: float32 [1024], replicated, may hold values from -0.1875 to 0.1875
- second_bias: float32 [1], replicated, may hold values from -3 to 3
Outputs:
- loss: float32 [2], P('group'), parts along dimension 0
- grad_first: float32 [262144, 1024], P(('group', 'tm')), parts along dimension 0
- grad_bias: float32 [2048], P('group'), parts along dimension 0
- grad_second: float32 [2048], P('group'), parts along dimension 0
- grad_out_bias: float32 [2], P('group'), parts along dimension 0
There are 2 independent parts, one for each index of `group`. A program takes and returns all parts, laid end to end along the dimension named above; an argument that names none is the same for every part. Nothing has to cross between parts.
All inputs are finite; a program needn't handle non-finite values.
Results may differ from a plain program's by a relative error of at most 0.0079.
Values may be sent and summed in bfloat16 or wider, within the bound.
No kernel may reach another device: no remote copies, remote signals or barrier semaphores. Data moves between devices by JAX's collectives and lax.ppermute only.
A program may use at most 192 MiB of HBM per device.

v0:
```python
import math

import jax
import jax.numpy as jnp
from jax import lax
from jax.sharding import PartitionSpec as P

N1 = 512
N2 = 512


def first_table(count):
    rows = jnp.arange(count, dtype=jnp.int32)[:, None]
    cols = jnp.arange(count, dtype=jnp.int32)[None, :]
    angle = 2.0 * math.pi / count * (rows * cols % count).astype(jnp.float32)
    scale = 1.0 / math.sqrt(count)
    return jnp.concatenate([jnp.cos(angle) * scale, -jnp.sin(angle) * scale], 0).astype(
        jnp.bfloat16
    )


def second_table(count):
    rows = jnp.arange(count, dtype=jnp.int32)[:, None]
    cols = jnp.arange(count // 2, dtype=jnp.int32)[None, :]
    angle = 2.0 * math.pi / count * (rows * cols % count).astype(jnp.float32)
    scale = 1.0 / math.sqrt(count)
    cosine = jnp.cos(angle) * scale
    sine = jnp.sin(angle) * scale
    upper = jnp.concatenate([cosine, -sine], 1)
    lower = jnp.concatenate([sine, cosine], 1)
    return jnp.concatenate([upper, lower], 0).astype(jnp.bfloat16)


def on_device(records, labels, first_weight, first_bias, second_weight, second_bias):
    devices = lax.axis_size("tm")
    slow_rows = N2 // devices
    fast_cols = N1 // devices
    table_one = first_table(N2)
    table_two = second_table(N1)
    total_len = N1 * N2
    count_rec = records.shape[0]
    samples = records.astype(jnp.bfloat16).reshape(count_rec, slow_rows, N1)
    samples = jnp.transpose(samples, (0, 2, 1))
    partial_value = jnp.einsum(
        "rcn,kn->rck",
        lax.all_to_all(samples, "tm", split_axis=1, concat_axis=2, tiled=True),
        table_one,
        preferred_element_type=jnp.float32,
    )
    real_part = partial_value[:, :, :N2]
    imag_part = partial_value[:, :, N2:]
    fast = lax.axis_index("tm") * fast_cols + jnp.arange(fast_cols, dtype=jnp.int32)
    slow = jnp.arange(N2, dtype=jnp.int32)
    phase = (
        2.0 * math.pi / total_len * (fast[:, None] * slow[None, :] % total_len).astype(jnp.float32)
    )
    cosine = jnp.cos(phase)[None]
    sine = jnp.sin(phase)[None]
    twisted_re = real_part * cosine + imag_part * sine
    twisted_im = imag_part * cosine - real_part * sine
    stacked = jnp.stack([twisted_re, twisted_im], 1).astype(jnp.bfloat16)
    twisted = jnp.transpose(stacked, (0, 3, 1, 2))
    block = lax.all_to_all(twisted, "tm", split_axis=1, concat_axis=3, tiled=True)
    count = block.shape[0]
    joined = block.reshape(count, block.shape[1], 2 * N1)
    bins = jnp.einsum("rbm,mf->rbf", joined, table_two, preferred_element_type=jnp.float32)
    power = bins[:, :, : N1 // 2] ** 2 + bins[:, :, N1 // 2 :] ** 2
    features = jnp.log(1.0 + power).astype(jnp.bfloat16).reshape(count, block.shape[1] * (N1 // 2))
    target = labels.astype(jnp.float32)
    partial_sums = jnp.dot(features, first_weight, preferred_element_type=jnp.float32)
    pre = lax.psum(partial_sums, "tm") + first_bias[None, :]
    gate = jax.nn.sigmoid(pre)
    hidden = pre * gate
    logit = jnp.sum(hidden * second_weight[None, :], 1) + second_bias[0]
    dlogit = jax.nn.sigmoid(logit) - target
    dpre = (dlogit[:, None] * second_weight[None, :] * gate * (1.0 + pre * (1.0 - gate))).astype(
        jnp.bfloat16
    )
    grad_first = lax.dot_general(
        features, dpre, (((0,), (0,)), ((), ())), preferred_element_type=jnp.float32
    )
    grad_bias = jnp.sum(dpre.astype(jnp.float32), 0)
    grad_second = jnp.sum(hidden * dlogit[:, None], 0)
    loss = jnp.mean(jnp.log(1.0 + jnp.exp(logit)) - target * logit).reshape(1)
    grad_out_bias = jnp.sum(dlogit).reshape(1)
    return (loss, grad_first, grad_bias, grad_second, grad_out_bias)


def solution(mesh):
    return jax.shard_map(
        on_device,
        mesh=mesh,
        in_specs=(P("group", "tm"), P("group"), P("tm", None), P(), P(), P()),
        out_specs=(P("group"), P(("group", "tm"), None), P("group"), P("group"), P("group")),
        check_vma=False,
    )
```

profile of v0, /device:TPU:0, one launch (start us, length us, event | category | flops | bytes accessed | tf_op | source)
XLA Modules:
  0.0 488.0 jit_solution(15323579355672855773)
XLA Ops:
  7.2 7.2 %copy.31 = bf16[128,16384]{0,1:T(8,128)(2,1)} copy(f32[128,16384]{1,0:T(8,128)} %param.6) | data formatting | bytes 12582912 | tf_op args[0]
  14.4 6.9 %copy.32 = bf16[128,512,32]{0,2,1:T(8,128)(2,1)} copy(bf16[128,512,32]{0,1,2:T(8,128)(2,1)} %bitcast.39) | data formatting | bytes 8388608 | tf_op jit(solution)/shard_map/transpose | solution.py:43
  21.2 7.4 %all-to-all-start = ((bf16[128,512,32]{0,2,1:T(8,128)(2,1)}), bf16[128,512,32]{0,2,1:T(8,128)(2,1)}, u32[]{:S(2)}, u32[]{:S(2)}) async-start(bf16[128,512,32]{0,2,1:T(8,128)(2,1)} %copy.32), calls=%async_computation | async-start | bytes 8388608 | tf_op jit(solution)/shard_map/all_to_all | solution.py:46
  28.7 4.4 multiply_convert_fusion
  33.1 0.3 fusion.36
  33.5 72.9 %all-to-all-done = bf16[128,512,32]{0,2,1:T(8,128)(2,1)} async-done(((bf16[128,512,32]{0,2,1:T(8,128)(2,1)}), bf16[128,512,32]{0,2,1:T(8,128)(2,1)}, u32[]{:S(2)}, u32[]{:S(2)}) %all-to-all-start) | async-done | bytes 4194336 | tf_op jit(solution)/shard_map/all_to_all | solution.py:46
  106.4 3.4 copy.33
  109.8 4.5 convolution_bitcast_fusion
  114.3 5.8 %fusion = (bf16[128,1,32,512]{0,3,2,1:T(8,128)(2,1)S(1)}, bf16[128,1,32,512]{0,3,2,1:T(8,128)(2,1)}) fusion(f32[128,32,1024]{0,2,1:T(8,128)S(1)} %convolution_bitcast_fusion, f32[32,512]{1,0:T(8,128)S(1)} %get-tuple-element.14, f32[32,512]{1,0:T(8,128)S(1)} %get-tuple-element.13), kind=kLoop, calls=%fused_computation.4 | loop fusion | flops 16777216 | bytes 25296896 | tf_op jit(solution)/shard_map/stack | solution.py:61
  120.2 6.3 %maximum_bitcast_fusion = bf16[128,512,2,32]{0,1,3,2:T(8,128)(2,1)} fusion(bf16[128,1,32,512]{0,3,2,1:T(8,128)(2,1)} %get-tuple-element.10, bf16[128,1,32,512]{0,3,2,1:T(8,128)(2,1)S(1)} %get-tuple-element.9), kind=kLoop, calls=%fused_computation.1 | loop fusion | flops 4194304 | bytes 16777216 | tf_op jit(solution)/shard_map/transpose | solution.py:62
  126.5 12.0 %copy.35 = bf16[128,512,2,32]{0,3,2,1:T(8,128)(2,1)} copy(bf16[128,512,2,32]{0,1,3,2:T(8,128)(2,1)} %maximum_bitcast_fusion) | data formatting | bytes 16777216 | tf_op jit(solution)/shard_map/transpose | solution.py:62
  138.5 19.7 %all-to-all-start.1 = ((bf16[128,512,2,32]{0,3,2,1:T(8,128)(2,1)}), bf16[128,512,2,32]{0,3,2,1:T(8,128)(2,1)}, u32[]{:S(2)}, u32[]{:S(2)}) async-start(bf16[128,512,2,32]{0,3,2,1:T(8,128)(2,1)} %copy.35), calls=%async_computation.1 | async-start | bytes 16777216 | tf_op jit(solution)/shard_map/all_to_all | solution.py:63
  158.2 0.0 all-reduce.2.cloned.1.call-start
  158.3 2.2 fusion.28
  160.5 2.2 negate_convert_fusion
  162.7 146.2 %all-to-all-done.1 = bf16[128,512,2,32]{0,3,2,1:T(8,128)(2,1)} async-done(((bf16[128,512,2,32]{0,3,2,1:T(8,128)(2,1)}), bf16[128,512,2,32]{0,3,2,1:T(8,128)(2,1)}, u32[]{:S(2)}, u32[]{:S(2)}) %all-to-all-start.1) | async-done | bytes 8388640 | tf_op jit(solution)/shard_map/all_to_all | solution.py:63
  308.9 9.0 %copy.36 = bf16[128,32,2,16,32]{0,4,3,2,1:T(8,128)(2,1)} copy(bf16[128,32,2,16,32]{0,4,2,1,3:T(8,128)(2,1)} %bitcast.11) | data formatting | bytes 16777216 | tf_op jit(solution)/shard_map/all_to_all | solution.py:63
  317.9 7.0 %fusion.11 = f32[128,32,512]{2,0,1:T(8,128)S(1)} fusion(bf16[128,32,1024]{0,2,1:T(8,128)(2,1)} %bitcast.36, bf16[512,256]{1,0:T(8,128)(2,1)S(1)} %get-tuple-element.18, bf16[512,256]{1,0:T(8,128)(2,1)S(1)} %fusion.28, bf16[512,256]{1,0:T(8,128)(2,1)S(1)} %get-tuple-element.17), kind=kOutput, calls=%fused_computation.22 | convolution fusion | flops 4299161600 | bytes 17563648 | tf_op jit(solution)/shard_map/rbm,mf->rbf/dot_general | solution.py:66
  324.9 2.3 fusion.5
  327.2 3.2 copy.38
  330.4 0.0 copy-start
  330.4 0.0 copy-start.1
  330.4 0.0 copy-start.2
  330.4 8.9 %fusion.40 = f32[128,1024]{1,0:T(8,128)} fusion(bf16[128,8192]{0,1:T(8,128)(2,1)S(1)} %bitcast.37, bf16[8192,1024]{1,0:T(8,128)(2,1)} %param.8), kind=kOutput, calls=%fused_computation.70 | convolution fusion | flops 2147483648 | bytes 19398656 | tf_op jit(solution)/shard_map/dot_general | solution.py:70
  339.4 0.0 all-reduce.2.cloned.1.call-update
  340.0 121.4 %all-reduce.2.cloned.1.call-done = f32[128,1024]{1,0:T(8,128)} async-done(((f32[128,1024]{1,0:T(8,128)}), f32[128,1024]{1,0:T(8,128)}) %all-reduce.2.cloned.1.call-update) | async-done | bytes 524304 | tf_op jit(solution)/shard_map/psum | solution.py:71
  461.4 0.0 copy-done
  461.4 1.3 multiply_reduce_fusion.1
  462.7 0.0 copy-done.2
  462.7 0.7 fusion.39
  463.4 1.9 convert_reduce_fusion
  465.4 14.0 %fusion.41 = f32[8192,1024]{1,0:T(8,128)} fusion(bf16[128,8192]{0,1:T(8,128)(2,1)S(1)} %bitcast.38, bf16[128,1024]{1,0:T(8,128)(2,1)S(1)} %get-tuple-element.8), kind=kOutput, calls=%fused_computation.71 | convolution fusion | flops 2147483648 | bytes 35913728 | tf_op jit(solution)/shard_map/dot_general | solution.py:79
  (2 shorter events, 0.0 us)
Async XLA Ops:
  21.2 85.1 %all-to-all-start = ((bf16[128,512,32]{0,2,1:T(8,128)(2,1)}), bf16[128,512,32]{0,2,1:T(8,128)(2,1)}, u32[]{:S(2)}, u32[]{:S(2)}) async-start(bf16[128,512,32]{0,2,1:T(8,128)(2,1)} %copy.32), calls=%async_computation | async-start | bytes 8388608 | tf_op jit(solution)/shard_map/all_to_all | solution.py:46
  138.5 170.4 %all-to-all-start.1 = ((bf16[128,512,2,32]{0,3,2,1:T(8,128)(2,1)}), bf16[128,512,2,32]{0,3,2,1:T(8,128)(2,1)}, u32[]{:S(2)}, u32[]{:S(2)}) async-start(bf16[128,512,2,32]{0,3,2,1:T(8,128)(2,1)} %copy.35), calls=%async_computation.1 | async-start | bytes 16777216 | tf_op jit(solution)/shard_map/all_to_all | solution.py:63
  158.2 303.2 %all-reduce.2.cloned.1.call-start = ((), (), s32[]{:S(2)}) async-start(), calls=%async_computation.2 | async-start | bytes 1048576 | tf_op jit(solution)/shard_map/psum | solution.py:71
  330.4 131.0 %copy-start = (f32[1024]{0:T(1024)S(1)}, f32[1024]{0:T(1024)}, u32[]{:S(2)}) copy-start(f32[1024]{0:T(1024)} %param.10) | copy-start | bytes 12292
  330.4 131.0 %copy-start.1 = (f32[1024]{0:T(1024)S(1)}, f32[1024]{0:T(1024)}, u32[]{:S(2)}) copy-start(f32[1024]{0:T(1024)} %param.9) | copy-start | bytes 12292
  330.4 132.3 %copy-start.2 = (s32[128]{0:T(128)S(1)}, s32[128]{0:T(128)}, u32[]{:S(2)}) copy-start(s32[128]{0:T(128)} %param.7) | copy-start | bytes 1540
Sparse Core Ops, SparseCore 0:
  339.5 121.8 all-reduce.1
where the time goes:
time: 489 us; the launch traced here: 488 us
  waiting for transfers between devices  341 us (70%)
  local copies, waits for them, and re-layouts  41.7 us (9%)
  matrix products  34.5 us (7%)
  other arithmetic  27.5 us (6%)
  starting transfers between devices  27.2 us (6%)
  between operations  16.6 us (3%)
    all_to_all x1, waiting for transfers between devices, on_device(): lax.all_to_all(twisted, 'tm', split_axis=1, concat_axis=3, tiled=True)  146 us
    psum x1, waiting for transfers between devices, on_device(): pre = lax.psum(partial_sums, 'tm') + first_bias[None, :]  121 us
    all_to_all x1, waiting for transfers between devices, on_device(): lax.all_to_all(samples, 'tm', split_axis=1, concat_axis=2, tiled=True)  72.9 us
    all_to_all x1, starting transfers between devices, on_device(): lax.all_to_all(twisted, 'tm', split_axis=1, concat_axis=3, tiled=True)  19.7 us
    dot_general x1, matrix products, on_device(): lax.dot_general(features, dpre, (((0,), (0,)), ((), ())), preferred_eleme...  14 us
    transpose x1, local copies, waits for them, and re-layouts, on_device(): twisted = jnp.transpose(stacked, (0, 3, 1, 2))  12 us
  transfers between devices with their start and end apart: 3, of which 3 were waited for; matrix products, arithmetic and copies ran while one was open for 2% of the time, Pallas kernels for 0%

commit v1 on v0

v1 whole, which is shorter than its diff:
```python
import functools
import math

import jax
import jax.numpy as jnp
import numpy as np
from jax import lax
from jax.experimental import pallas as pl
from jax.experimental.pallas import tpu as pltpu
from jax.sharding import PartitionSpec as P

N1 = 512
N2 = 512
HALF = N1 // 2
LANES = 128
ROW_BLOCK = 8
VMEM_LIMIT = 50 * 2**20


def tables():
    rows = np.arange(N2)[:, None]
    cols = np.arange(N2)[None, :]
    angle = 2.0 * math.pi / N2 * (rows * cols % N2)
    scale = 1.0 / math.sqrt(N2)
    one = np.concatenate([np.cos(angle) * scale, -np.sin(angle) * scale], 0)
    angle = 2.0 * math.pi / N1 * (np.arange(N1)[:, None] * np.arange(HALF)[None, :] % N1)
    scale = 1.0 / math.sqrt(N1)
    cosine, sine = np.cos(angle) * scale, np.sin(angle) * scale
    two = np.concatenate(
        [np.concatenate([cosine, -sine], 1), np.concatenate([sine, cosine], 1)], 0
    )
    total = N1 * N2
    phase = 2.0 * math.pi / total * (np.arange(N2)[:, None] * np.arange(N1)[None, :] % total)
    return (
        jnp.asarray(one.astype(np.float32), jnp.bfloat16),
        jnp.asarray(np.cos(phase).astype(np.float32)),
        jnp.asarray(np.sin(phase).astype(np.float32)),
        jnp.asarray(two.astype(np.float32), jnp.bfloat16),
    )


def prepare_kernel(x_ref, o_ref):
    slow = o_ref.shape[1]
    pieces = N1 // LANES
    for rec in range(ROW_BLOCK):
        for piece in range(pieces):
            rows = pl.ds(piece * ROW_BLOCK + rec, slow, stride=pieces * ROW_BLOCK)
            o_ref[rec, :, piece * LANES : (piece + 1) * LANES] = x_ref[0, rows, :].astype(
                jnp.bfloat16
            )


def prepare(view, first_row, rows, slow):
    first = first_row // ROW_BLOCK
    return pl.pallas_call(
        prepare_kernel,
        grid=(rows // ROW_BLOCK,),
        in_specs=[pl.BlockSpec((1, view.shape[1], LANES), lambda i: (i + first, 0, 0))],
        out_specs=pl.BlockSpec((ROW_BLOCK, slow, N1), lambda i: (i, 0, 0)),
        out_shape=jax.ShapeDtypeStruct((rows, slow, N1), jnp.bfloat16),
        cost_estimate=pl.CostEstimate(
            flops=rows * slow * N1, bytes_accessed=rows * slow * N1 * 6, transcendentals=0
        ),
        name="prepare",
    )(view)


def spectrum_kernel(x_ref, one_ref, cos_ref, sin_ref, two_ref, o_ref, *, block):
    parts, _, slow, _ = o_ref.shape
    data = x_ref[...].reshape(N2, N1)
    for start in range(0, N2, block):
        rows = slice(start, start + block)
        real = jnp.dot(one_ref[rows, :], data, preferred_element_type=jnp.float32)
        imag = jnp.dot(
            one_ref[N2 + start : N2 + start + block, :], data, preferred_element_type=jnp.float32
        )
        cosine = cos_ref[rows, :]
        sine = sin_ref[rows, :]
        twisted_re = (real * cosine + imag * sine).astype(jnp.bfloat16)
        twisted_im = (imag * cosine - real * sine).astype(jnp.bfloat16)
        bins = jnp.dot(twisted_re, two_ref[:N1, :], preferred_element_type=jnp.float32)
        bins += jnp.dot(twisted_im, two_ref[N1:, :], preferred_element_type=jnp.float32)
        power = bins[:, :HALF] ** 2 + bins[:, HALF:] ** 2
        feats = jnp.log(1.0 + power).astype(jnp.bfloat16)
        if parts == 1:
            o_ref[0, 0, rows, :] = feats
        else:
            o_ref[start // slow : (start + block) // slow, 0] = feats.reshape(
                block // slow, slow, HALF
            )


def spectrum(blocks, consts):
    parts, count, slow, _ = blocks.shape
    whole = lambda a: pl.BlockSpec(a.shape, lambda i: (0, 0))
    return pl.pallas_call(
        functools.partial(spectrum_kernel, block=max(128, slow)),
        grid=(count,),
        in_specs=[pl.BlockSpec((parts, 1, slow, N1), lambda i: (0, i, 0, 0))]
        + [whole(a) for a in consts],
        out_specs=pl.BlockSpec((parts, 1, slow, HALF), lambda i: (0, i, 0, 0)),
        out_shape=jax.ShapeDtypeStruct((parts, count, slow, HALF), jnp.bfloat16),
        compiler_params=pltpu.CompilerParams(vmem_limit_bytes=VMEM_LIMIT),
        cost_estimate=pl.CostEstimate(
            flops=count * 8 * N1 * N2 * N2,
            bytes_accessed=count * N1 * N2 * 3 + 4 * 2**20,
            transcendentals=count * N2 * HALF,
        ),
        name="spectrum",
    )(blocks, *consts)


def sum_over(value, devices):
    bit = 1
    while bit < devices:
        pairs = [(i, i ^ bit) for i in range(devices)]
        value = value + lax.ppermute(value, "tm", pairs)
        bit *= 2
    return value


def on_device(records, labels, first_weight, first_bias, second_weight, second_bias):
    devices = lax.axis_size("tm")
    count, local = records.shape
    slow = local // N1
    each = count // devices
    chunks = {8: (4,4)}.get(each, (each,))
    aligned = slow % 16 == 0
    consts = tables()
    pieces = N1 // LANES
    view = (
        records.reshape(count // ROW_BLOCK, ROW_BLOCK, slow, pieces, LANES)
        .transpose(0, 2, 3, 1, 4)
        .reshape(count // ROW_BLOCK, slow * pieces * ROW_BLOCK, LANES)
    )

    feature_chunks, pre_chunks = [], []
    row = 0
    for size in chunks:
        rows = size * devices
        mine = prepare(view, row, rows, slow).reshape(devices, size, slow, N1)
        blocks = lax.all_to_all(mine, "tm", split_axis=0, concat_axis=0, tiled=True)
        if not aligned:
            blocks = blocks.transpose(1, 0, 2, 3).reshape(1, size, N2, N1)
        feats = spectrum(blocks, consts)
        if not aligned:
            feats = feats.reshape(size, devices, slow, HALF).transpose(1, 0, 2, 3)
        feats = lax.all_to_all(feats, "tm", split_axis=0, concat_axis=0, tiled=True)
        feats = feats.reshape(rows, slow * HALF)
        feature_chunks.append(feats)
        partial_sums = jnp.dot(feats, first_weight, preferred_element_type=jnp.float32)
        pre_chunks.append(sum_over(partial_sums, devices))
        row += rows
    features = jnp.concatenate(feature_chunks, 0)
    pre = jnp.concatenate(pre_chunks, 0) + first_bias[None, :]

    target = labels.astype(jnp.float32)
    gate = jax.nn.sigmoid(pre)
    hidden = pre * gate
    logit = jnp.sum(hidden * second_weight[None, :], 1) + second_bias[0]
    dlogit = jax.nn.sigmoid(logit) - target
    dpre = (dlogit[:, None] * second_weight[None, :] * gate * (1.0 + pre * (1.0 - gate))).astype(
        jnp.bfloat16
    )
    grad_first = lax.dot_general(
        features, dpre, (((0,), (0,)), ((), ())), preferred_element_type=jnp.float32
    )
    grad_bias = jnp.sum(dpre.astype(jnp.float32), 0)
    grad_second = jnp.sum(hidden * dlogit[:, None], 0)
    loss = jnp.mean(jnp.log(1.0 + jnp.exp(logit)) - target * logit).reshape(1)
    grad_out_bias = jnp.sum(dlogit).reshape(1)
    return (loss, grad_first, grad_bias, grad_second, grad_out_bias)


def solution(mesh):
    return jax.shard_map(
        on_device,
        mesh=mesh,
        in_specs=(P("group", "tm"), P("group"), P("tm", None), P(), P(), P()),
        out_specs=(P("group"), P(("group", "tm"), None), P("group"), P("group"), P("group")),
        check_vma=False,
    )
```

time: 489 us -> 245 us (0.50)
  waiting for transfers between devices: 341 us -> 120 us
  local copies, waits for them, and re-layouts: 41.7 us -> 1.28 us
  Pallas kernels: 0 us -> 34.2 us
  other arithmetic: 27.5 us -> 2.02 us
  starting transfers between devices: 27.2 us -> 51.7 us
  between operations: 16.6 us -> 3.21 us
    all_to_all x2 -> x4, waiting for transfers between devices: 219 us -> 91.2 us  [the longest x2 65.2 us: on_device(): blocks = lax.all_to_all(mine, 'tm', split_axis=0, concat_axis=0, tiled=True)]
    psum x1 -> x0, waiting for transfers between devices: 121 us -> none  [on_device(): pre = lax.psum(partial_sums, 'tm') + first_bias[None, :]]
    pallas_call x0 -> x4, Pallas kernels: none -> 34.2 us  [the longest x2 19.9 us: spectrum(): pl.pallas_call(functools.partial(spectrum_kernel, block=max(128, slow)),...]
    ppermute x0 -> x8, waiting for transfers between devices: none -> 28.5 us  [sum_over(): value = value + lax.ppermute(value, 'tm', pairs)]
    transpose x2 -> x0, local copies, waits for them, and re-layouts: 18.8 us -> none  [the longest x1 12 us: on_device(): twisted = jnp.transpose(stacked, (0, 3, 1, 2))]
    ppermute x0 -> x8, starting transfers between devices: none -> 14.9 us  [sum_over(): value = value + lax.ppermute(value, 'tm', pairs)]
    another operation x4 -> x0, other arithmetic: 14.7 us -> none
    all_to_all x2 -> x0, local copies, waits for them, and re-layouts: 12.4 us -> none  [the longest x1 8.97 us: on_device(): lax.all_to_all(twisted, 'tm', split_axis=1, concat_axis=3, tiled=True)]
  transfers between devices with their start and end apart: 3 -> 12, of which waited for: 3 -> 8; matrix products, arithmetic and copies ran while one was open for 2% -> 8% of each run, Pallas kernels for 0% -> 11%
where the time goes in v1:
time: 245 us; the launch traced here: 244 us
  waiting for transfers between devices  120 us (49%)
  starting transfers between devices  51.7 us (21%)
  Pallas kernels  34.2 us (14%)
  matrix products  31.7 us (13%)
  between operations  3.21 us (1%)
    all_to_all x2, waiting for transfers between devices, on_device(): blocks = lax.all_to_all(mine, 'tm', split_axis=0, concat_axis=0, tiled=True)  65.2 us
    ppermute x8, waiting for transfers between devices, sum_over(): value = value + lax.ppermute(value, 'tm', pairs)  28.5 us
    all_to_all x2, waiting for transfers between devices, on_device(): feats = lax.all_to_all(feats, 'tm', split_axis=0, concat_axis=0, tiled=True)  26 us
    pallas_call x2, Pallas kernels, spectrum(): pl.pallas_call(functools.partial(spectrum_kernel, block=max(128, slow)),...  19.9 us
    all_to_all x2, starting transfers between devices, on_device(): blocks = lax.all_to_all(mine, 'tm', split_axis=0, concat_axis=0, tiled=True)  18.7 us
    all_to_all x2, starting transfers between devices, on_device(): feats = lax.all_to_all(feats, 'tm', split_axis=0, concat_axis=0, tiled=True)  18.1 us
    dot_general x2, matrix products, on_device(): jnp.dot(feats, first_weight, preferred_element_type=jnp.float32)  17.6 us
    ppermute x8, starting transfers between devices, sum_over(): value = value + lax.ppermute(value, 'tm', pairs)  14.9 us
  transfers between devices with their start and end apart: 12, of which 8 were waited for; matrix products, arithmetic and copies ran while one was open for 8% of the time, Pallas kernels for 11%

profile of v1, /device:TPU:0, one launch (start us, length us, event | category | flops | bytes accessed | tf_op | source)
XLA Modules:
  0.0 243.8 jit_solution(8628185470245402476)
XLA Ops:
  0.6 7.2 %prepare.3 = bf16[64,32,512]{2,1,0:T(8,128)(2,1)} custom-call(f32[16,1024,128]{2,1,0:T(8,128)} %bitcast.22), custom_call_target="tpu_custom_call" | custom-call | flops 1048576 | bytes 6291456 | tf_op jit(solution)/shard_map/prepare/pallas_call | solution.py:55
  7.8 7.4 %all-to-all-start.2 = ((bf16[16,4,32,512]{3,2,1,0:T(8,128)(2,1)}), bf16[16,4,32,512]{3,2,1,0:T(8,128)(2,1)}, u32[]{:S(2)}, u32[]{:S(2)}) async-start(bf16[16,4,32,512]{3,2,1,0:T(8,128)(2,1)} %bitcast.29), calls=%async_computation.2 | async-start | bytes 4194304 | tf_op jit(solution)/shard_map/all_to_all | solution.py:142
  15.2 7.1 %prepare.2 = bf16[64,32,512]{2,1,0:T(8,128)(2,1)} custom-call(f32[16,1024,128]{2,1,0:T(8,128)} %bitcast.23), custom_call_target="tpu_custom_call" | custom-call | flops 1048576 | bytes 6291456 | tf_op jit(solution)/shard_map/prepare/pallas_call | solution.py:55
  22.4 34.0 %all-to-all-done.2.x_ref = bf16[16,4,32,512]{3,2,1,0:T(8,128)(2,1)} async-done(((bf16[16,4,32,512]{3,2,1,0:T(8,128)(2,1)}), bf16[16,4,32,512]{3,2,1,0:T(8,128)(2,1)}, u32[]{:S(2)}, u32[]{:S(2)}) %all-to-all-start.2) | async-done | bytes 2097184 | tf_op jit(solution)/shard_map/all_to_all | solution.py:142
  56.4 11.3 %all-to-all-start = ((bf16[16,4,32,512]{3,2,1,0:T(8,128)(2,1)}), bf16[16,4,32,512]{3,2,1,0:T(8,128)(2,1)}, u32[]{:S(2)}, u32[]{:S(2)}) async-start(bf16[16,4,32,512]{3,2,1,0:T(8,128)(2,1)} %bitcast.28), calls=%async_computation | async-start | bytes 4194304 | tf_op jit(solution)/shard_map/all_to_all | solution.py:142
  67.7 9.9 %spectrum.3 = bf16[16,4,32,256]{3,2,1,0:T(8,128)(2,1)} custom-call(bf16[16,4,32,512]{3,2,1,0:T(8,128)(2,1)} %all-to-all-done.2.x_ref, bf16[1024,512]{1,0:T(8,128)(2,1)S(1)} %copy-done.1, f32[512,512]{1,0:T(8,128)S(1)} %copy-done, f32[512,512]{1,0:T(8,128)} %constant.18.clone.sin_ref, bf16[1024,512]{1,0:T(8,128)(2,1)} %constant.19.clone.two_ref), custom_call_target="tpu_custom_call" | custom-call | flops 4294967296 | bytes 7340032 | tf_op jit(solution)/shard_map/spectrum/pallas_call | solution.py:96
  77.6 31.2 %all-to-all-done.x_ref = bf16[16,4,32,512]{3,2,1,0:T(8,128)(2,1)} async-done(((bf16[16,4,32,512]{3,2,1,0:T(8,128)(2,1)}), bf16[16,4,32,512]{3,2,1,0:T(8,128)(2,1)}, u32[]{:S(2)}, u32[]{:S(2)}) %all-to-all-start) | async-done | bytes 2097184 | tf_op jit(solution)/shard_map/all_to_all | solution.py:142
  108.8 11.2 %all-to-all-start.3 = ((bf16[16,4,32,256]{3,2,1,0:T(8,128)(2,1)}), bf16[16,4,32,256]{3,2,1,0:T(8,128)(2,1)S(1)}, u32[]{:S(2)}, u32[]{:S(2)}) async-start(bf16[16,4,32,256]{3,2,1,0:T(8,128)(2,1)} %spectrum.3), calls=%async_computation.3 | async-start | bytes 2097152 | tf_op jit(solution)/shard_map/all_to_all | solution.py:148
  120.0 10.0 %spectrum.2 = bf16[16,4,32,256]{3,2,1,0:T(8,128)(2,1)} custom-call(bf16[16,4,32,512]{3,2,1,0:T(8,128)(2,1)} %all-to-all-done.x_ref, bf16[1024,512]{1,0:T(8,128)(2,1)S(1)} %copy-done.1, f32[512,512]{1,0:T(8,128)S(1)} %copy-done, f32[512,512]{1,0:T(8,128)} %constant.18.clone.sin_ref, bf16[1024,512]{1,0:T(8,128)(2,1)} %constant.19.clone.two_ref), custom_call_target="tpu_custom_call" | custom-call | flops 4294967296 | bytes 7340032 | tf_op jit(solution)/shard_map/spectrum/pallas_call | solution.py:96
  130.0 13.0 %all-to-all-done.3 = bf16[16,4,32,256]{3,2,1,0:T(8,128)(2,1)S(1)} async-done(((bf16[16,4,32,256]{3,2,1,0:T(8,128)(2,1)}), bf16[16,4,32,256]{3,2,1,0:T(8,128)(2,1)S(1)}, u32[]{:S(2)}, u32[]{:S(2)}) %all-to-all-start.3) | async-done | bytes 1048608 | tf_op jit(solution)/shard_map/all_to_all | solution.py:148
  143.0 6.9 %all-to-all-start.1 = ((bf16[16,4,32,256]{3,2,1,0:T(8,128)(2,1)}), bf16[16,4,32,256]{3,2,1,0:T(8,128)(2,1)S(1)}, u32[]{:S(2)}, u32[]{:S(2)}) async-start(bf16[16,4,32,256]{3,2,1,0:T(8,128)(2,1)} %spectrum.2), calls=%async_computation.1 | async-start | bytes 2097152 | tf_op jit(solution)/shard_map/all_to_all | solution.py:148
  149.9 0.6 copy.16
  150.5 8.8 %fusion.9 = f32[64,1024]{1,0:T(8,128)S(1)} fusion(bf16[64,8192]{1,0:T(8,128)(2,1)S(1)} %bitcast.24, bf16[8192,1024]{1,0:T(8,128)(2,1)} %param.12), kind=kOutput, calls=%fused_computation.16 | convolution fusion | flops 1073741824 | bytes 18087936 | tf_op jit(solution)/shard_map/dot_general | solution.py:151
  159.3 0.5 collective-permute-start.4
  159.8 13.0 %all-to-all-done.1 = bf16[16,4,32,256]{3,2,1,0:T(8,128)(2,1)S(1)} async-done(((bf16[16,4,32,256]{3,2,1,0:T(8,128)(2,1)}), bf16[16,4,32,256]{3,2,1,0:T(8,128)(2,1)S(1)}, u32[]{:S(2)}, u32[]{:S(2)}) %all-to-all-start.1) | async-done | bytes 1048608 | tf_op jit(solution)/shard_map/all_to_all | solution.py:148
  172.8 0.6 copy.15
  173.4 8.8 %fusion.8 = f32[64,1024]{1,0:T(8,128)S(1)} fusion(bf16[64,8192]{1,0:T(8,128)(2,1)S(1)} %bitcast.26, bf16[8192,1024]{1,0:T(8,128)(2,1)} %param.12), kind=kOutput, calls=%fused_computation.15 | convolution fusion | flops 1073741824 | bytes 18087936 | tf_op jit(solution)/shard_map/dot_general | solution.py:151
  182.3 0.7 collective-permute-start
  183.0 2.0 collective-permute-start.5
  185.1 1.1 collective-permute-start.1
  186.2 6.0 %collective-permute-done.5 = f32[64,1024]{1,0:T(8,128)S(1)} collective-permute-done((f32[64,1024]{1,0:T(8,128)S(1)}, f32[64,1024]{1,0:T(8,128)S(1)}, u32[]{:S(2)}, u32[]{:S(2)}) %collective-permute-start.5) | collective-permute-done | bytes 262176 | tf_op jit(solution)/shard_map/ppermute | solution.py:117
  192.2 3.5 %collective-permute-start.6 = (f32[64,1024]{1,0:T(8,128)S(1)}, f32[64,1024]{1,0:T(8,128)S(1)}, u32[]{:S(2)}, u32[]{:S(2)}) collective-permute-start(f32[64,1024]{1,0:T(8,128)S(1)} %add.55), channel_id=1, source_target_pairs={{0,4},{1,5},{2,6},{3,7},{4,0},{5,1},{6,2},{7,3},{8,12},{9,13},{10,... | collective-permute-start | bytes 786440 | tf_op jit(solution)/shard_map/ppermute | solution.py:117
  195.7 1.4 collective-permute-done.1
  197.2 3.2 %collective-permute-start.2 = (f32[64,1024]{1,0:T(8,128)S(1)}, f32[64,1024]{1,0:T(8,128)S(1)}, u32[]{:S(2)}, u32[]{:S(2)}) collective-permute-start(f32[64,1024]{1,0:T(8,128)S(1)} %add.51), channel_id=1, source_target_pairs={{0,4},{1,5},{2,6},{3,7},{4,0},{5,1},{6,2},{7,3},{8,12},{9,13},{10,... | collective-permute-start | bytes 786440 | tf_op jit(solution)/shard_map/ppermute | solution.py:117
  200.5 3.9 %collective-permute-start.7 = (f32[64,1024]{1,0:T(8,128)S(1)}, f32[64,1024]{1,0:T(8,128)S(1)}, u32[]{:S(2)}, u32[]{:S(2)}) collective-permute-start(f32[64,1024]{1,0:T(8,128)S(1)} %add.56), channel_id=1, source_target_pairs={{0,8},{1,9},{2,10},{3,11},{4,12},{5,13},{6,14},{7,15},{8,0},{9,1},... | collective-permute-start | bytes 786440 | tf_op jit(solution)/shard_map/ppermute | solution.py:117
  204.4 7.3 %collective-permute-done.2 = f32[64,1024]{1,0:T(8,128)S(1)} collective-permute-done((f32[64,1024]{1,0:T(8,128)S(1)}, f32[64,1024]{1,0:T(8,128)S(1)}, u32[]{:S(2)}, u32[]{:S(2)}) %collective-permute-start.2) | collective-permute-done | bytes 262176 | tf_op jit(solution)/shard_map/ppermute | solution.py:117
  211.7 0.1 collective-permute-start.3
  212.5 13.7 %collective-permute-done.3 = f32[64,1024]{1,0:T(8,128)S(1)} collective-permute-done((f32[64,1024]{1,0:T(8,128)S(1)}, f32[64,1024]{1,0:T(8,128)S(1)}, u32[]{:S(2)}, u32[]{:S(2)}) %collective-permute-start.3) | collective-permute-done | bytes 262176 | tf_op jit(solution)/shard_map/ppermute | solution.py:117
  226.2 0.2 multiply_reduce_fusion.1
  226.5 0.7 fusion.6
  227.1 0.9 convert_reduce_fusion
  228.0 14.1 %fusion = f32[8192,1024]{1,0:T(8,128)} fusion(bf16[128,1024]{1,0:T(8,128)(2,1)S(1)} %get-tuple-element.8, bf16[64,8192]{1,0:T(8,128)(2,1)S(1)} %bitcast.25, bf16[64,8192]{1,0:T(8,128)(2,1)S(1)} %bitcast.27), kind=kOutput, calls=%fused_computation | convolution fusion | flops 2151677952 | bytes 35913728 | tf_op jit(solution)/shard_map/dot_general | solution.py:165
  (22 shorter events, 0.3 us)
Async XLA Ops:
  7.8 48.6 %all-to-all-start.2 = ((bf16[16,4,32,512]{3,2,1,0:T(8,128)(2,1)}), bf16[16,4,32,512]{3,2,1,0:T(8,128)(2,1)}, u32[]{:S(2)}, u32[]{:S(2)}) async-start(bf16[16,4,32,512]{3,2,1,0:T(8,128)(2,1)} %bitcast.29), calls=%async_computation.2 | async-start | bytes 4194304 | tf_op jit(solution)/shard_map/all_to_all | solution.py:142
  22.4 45.3 %copy-start = (f32[512,512]{1,0:T(8,128)S(1)}, f32[512,512]{1,0:T(8,128)}, u32[]{:S(2)}) copy-start(f32[512,512]{1,0:T(8,128)} %constant.17.clone.cos_ref) | copy-start | bytes 3145732
  22.4 45.3 %copy-start.1 = (bf16[1024,512]{1,0:T(8,128)(2,1)S(1)}, bf16[1024,512]{1,0:T(8,128)(2,1)}, u32[]{:S(2)}) copy-start(bf16[1024,512]{1,0:T(8,128)(2,1)} %constant.16.clone.one_ref) | copy-start | bytes 3145732
  56.4 52.4 %all-to-all-start = ((bf16[16,4,32,512]{3,2,1,0:T(8,128)(2,1)}), bf16[16,4,32,512]{3,2,1,0:T(8,128)(2,1)}, u32[]{:S(2)}, u32[]{:S(2)}) async-start(bf16[16,4,32,512]{3,2,1,0:T(8,128)(2,1)} %bitcast.28), calls=%async_computation | async-start | bytes 4194304 | tf_op jit(solution)/shard_map/all_to_all | solution.py:142
  108.8 34.2 %all-to-all-start.3 = ((bf16[16,4,32,256]{3,2,1,0:T(8,128)(2,1)}), bf16[16,4,32,256]{3,2,1,0:T(8,128)(2,1)S(1)}, u32[]{:S(2)}, u32[]{:S(2)}) async-start(bf16[16,4,32,256]{3,2,1,0:T(8,128)(2,1)} %spectrum.3), calls=%async_computation.3 | async-start | bytes 2097152 | tf_op jit(solution)/shard_map/all_to_all | solution.py:148
  143.0 29.8 %all-to-all-start.1 = ((bf16[16,4,32,256]{3,2,1,0:T(8,128)(2,1)}), bf16[16,4,32,256]{3,2,1,0:T(8,128)(2,1)S(1)}, u32[]{:S(2)}, u32[]{:S(2)}) async-start(bf16[16,4,32,256]{3,2,1,0:T(8,128)(2,1)} %spectrum.2), calls=%async_computation.1 | async-start | bytes 2097152 | tf_op jit(solution)/shard_map/all_to_all | solution.py:148
  159.3 23.7 %collective-permute-start.4 = (f32[64,1024]{1,0:T(8,128)S(1)}, f32[64,1024]{1,0:T(8,128)S(1)}, u32[]{:S(2)}, u32[]{:S(2)}) collective-permute-start(f32[64,1024]{1,0:T(8,128)S(1)} %fusion.9), channel_id=1, source_target_pairs={{0,1},{1,0},{2,3},{3,2},{4,5},{5,4},{6,7},{7,6},{8,9},{9,8},{10,11... | collective-permute-start | bytes 786440 | tf_op jit(solution)/shard_map/ppermute | solution.py:117
  182.3 43.9 %copy-start.2 = (f32[1024]{0:T(1024)S(1)}, f32[1024]{0:T(1024)}, u32[]{:S(2)}) copy-start(f32[1024]{0:T(1024)} %param.14) | copy-start | bytes 12292
  182.3 43.9 %copy-start.3 = (f32[1024]{0:T(1024)S(1)}, f32[1024]{0:T(1024)}, u32[]{:S(2)}) copy-start(f32[1024]{0:T(1024)} %param.13) | copy-start | bytes 12292
  182.3 44.2 %copy-start.4 = (s32[128]{0:T(128)S(1)}, s32[128]{0:T(128)}, u32[]{:S(2)}) copy-start(s32[128]{0:T(128)} %param.11) | copy-start | bytes 1540
  182.3 2.7 %collective-permute-start = (f32[64,1024]{1,0:T(8,128)S(1)}, f32[64,1024]{1,0:T(8,128)S(1)}, u32[]{:S(2)}, u32[]{:S(2)}) collective-permute-start(f32[64,1024]{1,0:T(8,128)S(1)} %fusion.8), channel_id=1, source_target_pairs={{0,1},{1,0},{2,3},{3,2},{4,5},{5,4},{6,7},{7,6},{8,9},{9,8},{10,11... | collective-permute-start | bytes 786440 | tf_op jit(solution)/shard_map/ppermute | solution.py:117
  183.0 9.2 %collective-permute-start.5 = (f32[64,1024]{1,0:T(8,128)S(1)}, f32[64,1024]{1,0:T(8,128)S(1)}, u32[]{:S(2)}, u32[]{:S(2)}) collective-permute-start(f32[64,1024]{1,0:T(8,128)S(1)} %add.54), channel_id=1, source_target_pairs={{0,2},{1,3},{2,0},{3,1},{4,6},{5,7},{6,4},{7,5},{8,10},{9,11},{10,... | collective-permute-start | bytes 786440 | tf_op jit(solution)/shard_map/ppermute | solution.py:117
  185.1 12.1 %collective-permute-start.1 = (f32[64,1024]{1,0:T(8,128)S(1)}, f32[64,1024]{1,0:T(8,128)S(1)}, u32[]{:S(2)}, u32[]{:S(2)}) collective-permute-start(f32[64,1024]{1,0:T(8,128)S(1)} %add.50), channel_id=1, source_target_pairs={{0,2},{1,3},{2,0},{3,1},{4,6},{5,7},{6,4},{7,5},{8,10},{9,11},{10,... | collective-permute-start | bytes 786440 | tf_op jit(solution)/shard_map/ppermute | solution.py:117
  192.2 8.2 %collective-permute-start.6 = (f32[64,1024]{1,0:T(8,128)S(1)}, f32[64,1024]{1,0:T(8,128)S(1)}, u32[]{:S(2)}, u32[]{:S(2)}) collective-permute-start(f32[64,1024]{1,0:T(8,128)S(1)} %add.55), channel_id=1, source_target_pairs={{0,4},{1,5},{2,6},{3,7},{4,0},{5,1},{6,2},{7,3},{8,12},{9,13},{10,... | collective-permute-start | bytes 786440 | tf_op jit(solution)/shard_map/ppermute | solution.py:117
  197.2 14.5 %collective-permute-start.2 = (f32[64,1024]{1,0:T(8,128)S(1)}, f32[64,1024]{1,0:T(8,128)S(1)}, u32[]{:S(2)}, u32[]{:S(2)}) collective-permute-start(f32[64,1024]{1,0:T(8,128)S(1)} %add.51), channel_id=1, source_target_pairs={{0,4},{1,5},{2,6},{3,7},{4,0},{5,1},{6,2},{7,3},{8,12},{9,13},{10,... | collective-permute-start | bytes 786440 | tf_op jit(solution)/shard_map/ppermute | solution.py:117
  200.5 12.0 %collective-permute-start.7 = (f32[64,1024]{1,0:T(8,128)S(1)}, f32[64,1024]{1,0:T(8,128)S(1)}, u32[]{:S(2)}, u32[]{:S(2)}) collective-permute-start(f32[64,1024]{1,0:T(8,128)S(1)} %add.56), channel_id=1, source_target_pairs={{0,8},{1,9},{2,10},{3,11},{4,12},{5,13},{6,14},{7,15},{8,0},{9,1},... | collective-permute-start | bytes 786440 | tf_op jit(solution)/shard_map/ppermute | solution.py:117
  211.7 14.5 %collective-permute-start.3 = (f32[64,1024]{1,0:T(8,128)S(1)}, f32[64,1024]{1,0:T(8,128)S(1)}, u32[]{:S(2)}, u32[]{:S(2)}) collective-permute-start(f32[64,1024]{1,0:T(8,128)S(1)} %add.52), channel_id=1, source_target_pairs={{0,8},{1,9},{2,10},{3,11},{4,12},{5,13},{6,14},{7,15},{8,0},{9,1},... | collective-permute-start | bytes 786440 | tf_op jit(solution)/shard_map/ppermute | solution.py:117

commit v2 on v1

--- a/solution.py
+++ b/solution.py
@@ -22,66 +22,64 @@
     cols = np.arange(N2)[None, :]
     angle = 2.0 * math.pi / N2 * (rows * cols % N2)
     scale = 1.0 / math.sqrt(N2)
-    one = np.concatenate([np.cos(angle) * scale, -np.sin(angle) * scale], 0)
-    angle = 2.0 * math.pi / N1 * (np.arange(N1)[:, None] * np.arange(HALF)[None, :] % N1)
-    scale = 1.0 / math.sqrt(N1)
-    cosine, sine = np.cos(angle) * scale, np.sin(angle) * scale
-    two = np.concatenate(
-        [np.concatenate([cosine, -sine], 1), np.concatenate([sine, cosine], 1)], 0
-    )
+    table = np.concatenate([np.cos(angle) * scale, -np.sin(angle) * scale], 0)
     total = N1 * N2
-    phase = 2.0 * math.pi / total * (np.arange(N2)[:, None] * np.arange(N1)[None, :] % total)
-    return (
-        jnp.asarray(one.astype(np.float32), jnp.bfloat16),
-        jnp.asarray(np.cos(phase).astype(np.float32)),
-        jnp.asarray(np.sin(phase).astype(np.float32)),
-        jnp.asarray(two.astype(np.float32), jnp.bfloat16),
-    )
-
-
-def prepare_kernel(x_ref, o_ref):
+    slow = jnp.arange(N2, dtype=jnp.int32)[:, None]
+    fast = jnp.arange(N1, dtype=jnp.int32)[None, :]
+    phase = 2.0 * math.pi / total * (slow * fast % total).astype(jnp.float32)
+    return jnp.asarray(table.astype(np.float32), jnp.bfloat16), jnp.cos(phase), jnp.sin(phase)
+
+
+def prepare_kernel(*refs):
+    *x_refs, o_ref = refs
     slow = o_ref.shape[1]
-    pieces = N1 // LANES
-    for rec in range(ROW_BLOCK):
-        for piece in range(pieces):
-            rows = pl.ds(piece * ROW_BLOCK + rec, slow, stride=pieces * ROW_BLOCK)
-            o_ref[rec, :, piece * LANES : (piece + 1) * LANES] = x_ref[0, rows, :].astype(
-                jnp.bfloat16
-            )
+    step = math.gcd(slow, 16)
+    for eight, x_ref in enumerate(x_refs):
+        recs = slice(eight * ROW_BLOCK, (eight + 1) * ROW_BLOCK)
+        for start in range(0, slow, step):
+            rows = slice(start, start + step)
+            for piece in range(N1 // LANES):
+                value = x_ref[0, rows, piece].astype(jnp.bfloat16)
+                o_ref[recs, rows, piece * LANES : (piece + 1) * LANES] = jnp.swapaxes(value, 0, 1)
 
 
 def prepare(view, first_row, rows, slow):
     first = first_row // ROW_BLOCK
+    eights = rows // ROW_BLOCK
+    streams = next(s for s in (4, 3, 5, 2, 1) if eights % s == 0)
+    block = (1,) + view.shape[1:]
+    spec = lambda s: pl.BlockSpec(block, lambda i: (i * streams + s + first, 0, 0, 0, 0))
     return pl.pallas_call(
         prepare_kernel,
-        grid=(rows // ROW_BLOCK,),
-        in_specs=[pl.BlockSpec((1, view.shape[1], LANES), lambda i: (i + first, 0, 0))],
-        out_specs=pl.BlockSpec((ROW_BLOCK, slow, N1), lambda i: (i, 0, 0)),
+        grid=(eights // streams,),
+        in_specs=[spec(s) for s in range(streams)],
+        out_specs=pl.BlockSpec((streams * ROW_BLOCK, slow, N1), lambda i: (i, 0, 0)),
         out_shape=jax.ShapeDtypeStruct((rows, slow, N1), jnp.bfloat16),
+        compiler_params=pltpu.CompilerParams(vmem_limit_bytes=VMEM_LIMIT),
         cost_estimate=pl.CostEstimate(
             flops=rows * slow * N1, bytes_accessed=rows * slow * N1 * 6, transcendentals=0
         ),
         name="prepare",
-    )(view)
-
-
-def spectrum_kernel(x_ref, one_ref, cos_ref, sin_ref, two_ref, o_ref, *, block):
+    )(*[view] * streams)
+
+
+def spectrum_kernel(x_ref, table_ref, cos_ref, sin_ref, o_ref, *, block):
     parts, _, slow, _ = o_ref.shape
     data = x_ref[...].reshape(N2, N1)
+    dot = functools.partial(jnp.dot, preferred_element_type=jnp.float32)
     for start in range(0, N2, block):
         rows = slice(start, start + block)
-        real = jnp.dot(one_ref[rows, :], data, preferred_element_type=jnp.float32)
-        imag = jnp.dot(
-            one_ref[N2 + start : N2 + start + block, :], data, preferred_element_type=jnp.float32
-        )
+        real = dot(table_ref[rows, :], data)
+        imag = dot(table_ref[N2 + start : N2 + start + block, :], data)
         cosine = cos_ref[rows, :]
         sine = sin_ref[rows, :]
         twisted_re = (real * cosine + imag * sine).astype(jnp.bfloat16)
         twisted_im = (imag * cosine - real * sine).astype(jnp.bfloat16)
-        bins = jnp.dot(twisted_re, two_ref[:N1, :], preferred_element_type=jnp.float32)
-        bins += jnp.dot(twisted_im, two_ref[N1:, :], preferred_element_type=jnp.float32)
-        power = bins[:, :HALF] ** 2 + bins[:, HALF:] ** 2
-        feats = jnp.log(1.0 + power).astype(jnp.bfloat16)
+        table_cos = table_ref[:N1, :HALF]
+        minus_sin = table_ref[N1:, :HALF]
+        bins_re = dot(twisted_re, table_cos) - dot(twisted_im, minus_sin)
+        bins_im = dot(twisted_re, minus_sin) + dot(twisted_im, table_cos)
+        feats = jnp.log(1.0 + (bins_re**2 + bins_im**2)).astype(jnp.bfloat16)
         if parts == 1:
             o_ref[0, 0, rows, :] = feats
         else:
@@ -110,13 +108,42 @@
     )(blocks, *consts)
 
 
+def exchange(value, bit, devices):
+    return lax.ppermute(value, "tm", [(i, i ^ bit) for i in range(devices)])
+
+
 def sum_over(value, devices):
-    bit = 1
-    while bit < devices:
-        pairs = [(i, i ^ bit) for i in range(devices)]
-        value = value + lax.ppermute(value, "tm", pairs)
-        bit *= 2
-    return value
+    quarter = value.shape[1] // 4
+    if devices % 4:
+        bit = 1
+        while bit < devices:
+            value = value + exchange(value, bit, devices)
+            bit *= 2
+        return value
+    me = lax.axis_index("tm") % 4
+    part = [
+        lax.dynamic_slice_in_dim(value, (me ^ k) * quarter, quarter, 1) for k in range(4)
+    ]
+    got = [exchange(part[k], k, devices) for k in range(1, 4)]
+    own = (part[0] + got[0]) + (got[1] + got[2])
+    if devices == 16:
+        got = [exchange(own, 4 * k, devices) for k in range(1, 4)]
+        own = (own + got[0]) + (got[1] + got[2])
+    else:
+        bit = 4
+        while bit < devices:
+            own = own + exchange(own, bit, devices)
+            bit *= 2
+    got = [own] + [exchange(own, k, devices) for k in range(1, 4)]
+    odd = (me % 2) == 1
+    high = me >= 2
+    low_pair = [jnp.where(odd, got[1], got[0]), jnp.where(odd, got[0], got[1])]
+    high_pair = [jnp.where(odd, got[3], got[2]), jnp.where(odd, got[2], got[3])]
+    return jnp.concatenate(
+        [jnp.where(high, h, l) for l, h in zip(low_pair, high_pair)]
+        + [jnp.where(high, l, h) for l, h in zip(low_pair, high_pair)],
+        1,
+    )
 
 
 def on_device(records, labels, first_weight, first_bias, second_weight, second_bias):
@@ -124,14 +151,13 @@
     count, local = records.shape
     slow = local // N1
     each = count // devices
-    chunks = {8: (4,4)}.get(each, (each,))
+    chunks = {8: (3, 5)}.get(each, (each,))
     aligned = slow % 16 == 0
     consts = tables()
     pieces = N1 // LANES
     view = (
         records.reshape(count // ROW_BLOCK, ROW_BLOCK, slow, pieces, LANES)
         .transpose(0, 2, 3, 1, 4)
-        .reshape(count // ROW_BLOCK, slow * pieces * ROW_BLOCK, LANES)
     )
 
     feature_chunks, pre_chunks = [], []

time: 245 us -> 224 us (0.914)
  waiting for transfers between devices: 120 us -> 96.7 us
  Pallas kernels: 34.2 us -> 26.1 us
  other arithmetic: 2.02 us -> 5.98 us
  starting transfers between devices: 51.7 us -> 55.5 us
    ppermute x8 -> x18, waiting for transfers between devices: 28.5 us -> 8.77 us  [exchange(): return lax.ppermute(value, 'tm', [(i, i ^ bit) for i in range(devices)])]
    pallas_call x2, Pallas kernels: 14.3 us -> 7.05 us  [prepare(): pl.pallas_call(prepare_kernel, grid=(eights // streams,), in_specs=[spec(...]
    ppermute x8 -> x18, starting transfers between devices: 14.9 us -> 20 us  [exchange(): return lax.ppermute(value, 'tm', [(i, i ^ bit) for i in range(devices)])]
    all_to_all x2, waiting for transfers between devices: 26 us -> 21.4 us  [on_device(): feats = lax.all_to_all(feats, 'tm', split_axis=0, concat_axis=0, tiled=True)]
    sin x0 -> x1, other arithmetic: none -> 4.09 us  [tables(): jnp.sin(phase)]
  transfers between devices with their start and end apart: 12 -> 22, of which waited for: 8 -> 8; matrix products, arithmetic and copies ran while one was open for 8% -> 11% of each run, Pallas kernels for 11% -> 10%
where the time goes in v2:
time: 224 us; the launch traced here: 223 us
  waiting for transfers between devices  96.7 us (43%)
  starting transfers between devices  55.5 us (25%)
  matrix products  31.7 us (14%)
  Pallas kernels  26.1 us (12%)
  other arithmetic  5.98 us (3%)
  local copies, waits for them, and re-layouts  3.63 us (2%)
  between operations  3.27 us (1%)
    all_to_all x2, waiting for transfers between devices, on_device(): blocks = lax.all_to_all(mine, 'tm', split_axis=0, concat_axis=0, tiled=True)  66.5 us
    all_to_all x2, waiting for transfers between devices, on_device(): feats = lax.all_to_all(feats, 'tm', split_axis=0, concat_axis=0, tiled=True)  21.4 us
    ppermute x18, starting transfers between devices, exchange(): return lax.ppermute(value, 'tm', [(i, i ^ bit) for i in range(devices)])  20 us
    pallas_call x2, Pallas kernels, spectrum(): pl.pallas_call(functools.partial(spectrum_kernel, block=max(128, slow)),...  19.1 us
    all_to_all x2, starting transfers between devices, on_device(): feats = lax.all_to_all(feats, 'tm', split_axis=0, concat_axis=0, tiled=True)  18.8 us
    dot_general x2, matrix products, on_device(): jnp.dot(feats, first_weight, preferred_element_type=jnp.float32)  17.6 us
    all_to_all x2, starting transfers between devices, on_device(): blocks = lax.all_to_all(mine, 'tm', split_axis=0, concat_axis=0, tiled=True)  16.7 us
    dot_general x1, matrix products, on_device(): lax.dot_general(features, dpre, (((0,), (0,)), ((), ())), preferred_eleme...  14.1 us
  transfers between devices with their start and end apart: 22, of which 8 were waited for; matrix products, arithmetic and copies ran while one was open for 11% of the time, Pallas kernels for 10%

profile of v2, /device:TPU:0, one launch (start us, length us, event | category | flops | bytes accessed | tf_op | source)
XLA Modules:
  0.0 222.9 jit_solution(3030027061372866946)
XLA Ops:
  0.6 3.0 %prepare.2 = bf16[48,32,512]{2,1,0:T(8,128)(2,1)} custom-call(f32[16,32,4,8,128]{4,3,2,1,0:T(8,128)} %bitcast.20, f32[16,32,4,8,128]{4,3,2,1,0:T(8,128)} %bitcast.21, f32[16,32,4,8,128]{4,3,2,1,0:T(8,128)} %bitcast.22), custom_call_target="tpu_custom_call" | custom-call | flops 786432 | bytes 4718592 | tf_op jit(solution)/shard_map/prepare/pallas_call | solution.py:52
  3.7 7.4 %all-to-all-start = ((bf16[16,3,32,512]{3,2,1,0:T(8,128)(2,1)}), bf16[16,3,32,512]{3,2,1,0:T(8,128)(2,1)S(1)}, u32[]{:S(2)}, u32[]{:S(2)}) async-start(bf16[16,3,32,512]{3,2,1,0:T(8,128)(2,1)} %bitcast.2), calls=%async_computation | async-start | bytes 3145728 | tf_op jit(solution)/shard_map/all_to_all | solution.py:168
  11.1 4.0 %prepare.3 = bf16[80,32,512]{2,1,0:T(8,128)(2,1)} custom-call(f32[16,32,4,8,128]{4,3,2,1,0:T(8,128)} %bitcast.23, f32[16,32,4,8,128]{4,3,2,1,0:T(8,128)} %bitcast.24, f32[16,32,4,8,128]{4,3,2,1,0:T(8,128)} %bitcast.25, f32[16,32,4,8,128]{4,3,2,1,0:T(8,128)} %bitcast.26, f32[16,32,4,8,128]{4,3,2,1,0:T(8,128)} %bitcast.27), custom_call_target="tpu_custom_call" | custom-call | flops 1310720 | bytes 7864320 | tf_op jit(solution)/shard_map/prepare/pallas_call | solution.py:52
  15.1 28.0 %all-to-all-done.x_ref = bf16[16,3,32,512]{3,2,1,0:T(8,128)(2,1)S(1)} async-done(((bf16[16,3,32,512]{3,2,1,0:T(8,128)(2,1)}), bf16[16,3,32,512]{3,2,1,0:T(8,128)(2,1)S(1)}, u32[]{:S(2)}, u32[]{:S(2)}) %all-to-all-start) | async-done | bytes 1572896 | tf_op jit(solution)/shard_map/all_to_all | solution.py:168
  43.1 1.2 copy-done.1
  44.2 9.3 %all-to-all-start.2 = ((bf16[16,5,32,512]{3,2,1,0:T(8,128)(2,1)}), bf16[16,5,32,512]{3,2,1,0:T(8,128)(2,1)}, u32[]{:S(2)}, u32[]{:S(2)}) async-start(bf16[16,5,32,512]{3,2,1,0:T(8,128)(2,1)} %bitcast.4), calls=%async_computation.2 | async-start | bytes 5242880 | tf_op jit(solution)/shard_map/all_to_all | solution.py:168
  53.5 4.1 %fusion.11 = (f32[512,512]{1,0:T(8,128)S(1)}, f32[512,512]{1,0:T(8,128)S(1)}) fusion(), kind=kLoop, calls=%fused_computation.20 | loop fusion | flops 3670016 | bytes 2097152 | tf_op jit(solution)/shard_map/sin | solution.py:30
  57.6 7.6 %spectrum.2 = bf16[16,3,32,256]{3,2,1,0:T(8,128)(2,1)} custom-call(bf16[16,3,32,512]{3,2,1,0:T(8,128)(2,1)} %copy-done.1, bf16[1024,512]{1,0:T(8,128)(2,1)S(1)} %copy-done, f32[512,512]{1,0:T(8,128)S(1)} %get-tuple-element.28.cos_ref, f32[512,512]{1,0:T(8,128)S(1)} %get-tuple-element.27.sin_ref), custom_call_target="tpu_custom_call" | custom-call | flops 3221225472 | bytes 6553600 | tf_op jit(solution)/shard_map/spectrum/pallas_call | solution.py:94
  65.2 38.6 %all-to-all-done.2.x_ref = bf16[16,5,32,512]{3,2,1,0:T(8,128)(2,1)} async-done(((bf16[16,5,32,512]{3,2,1,0:T(8,128)(2,1)}), bf16[16,5,32,512]{3,2,1,0:T(8,128)(2,1)}, u32[]{:S(2)}, u32[]{:S(2)}) %all-to-all-start.2) | async-done | bytes 2621472 | tf_op jit(solution)/shard_map/all_to_all | solution.py:168
  103.8 13.4 %all-to-all-start.1 = ((bf16[16,3,32,256]{3,2,1,0:T(8,128)(2,1)}), bf16[16,3,32,256]{3,2,1,0:T(8,128)(2,1)}, u32[]{:S(2)}, u32[]{:S(2)}) async-start(bf16[16,3,32,256]{3,2,1,0:T(8,128)(2,1)} %spectrum.2), calls=%async_computation.1 | async-start | bytes 1572864 | tf_op jit(solution)/shard_map/all_to_all | solution.py:174
  117.2 11.5 %spectrum.3 = bf16[16,5,32,256]{3,2,1,0:T(8,128)(2,1)} custom-call(bf16[16,5,32,512]{3,2,1,0:T(8,128)(2,1)} %all-to-all-done.2.x_ref, bf16[1024,512]{1,0:T(8,128)(2,1)S(1)} %copy-done, f32[512,512]{1,0:T(8,128)S(1)} %get-tuple-element.28.cos_ref, f32[512,512]{1,0:T(8,128)S(1)} %get-tuple-element.27.sin_ref), custom_call_target="tpu_custom_call" | custom-call | flops 5368709120 | bytes 8126464 | tf_op jit(solution)/shard_map/spectrum/pallas_call | solution.py:94
  128.6 7.3 %all-to-all-done.1 = bf16[16,3,32,256]{3,2,1,0:T(8,128)(2,1)} async-done(((bf16[16,3,32,256]{3,2,1,0:T(8,128)(2,1)}), bf16[16,3,32,256]{3,2,1,0:T(8,128)(2,1)}, u32[]{:S(2)}, u32[]{:S(2)}) %all-to-all-start.1) | async-done | bytes 786464 | tf_op jit(solution)/shard_map/all_to_all | solution.py:174
  135.9 5.5 %all-to-all-start.3 = ((bf16[16,5,32,256]{3,2,1,0:T(8,128)(2,1)}), bf16[16,5,32,256]{3,2,1,0:T(8,128)(2,1)S(1)}, u32[]{:S(2)}, u32[]{:S(2)}) async-start(bf16[16,5,32,256]{3,2,1,0:T(8,128)(2,1)} %spectrum.3), calls=%async_computation.3 | async-start | bytes 2621440 | tf_op jit(solution)/shard_map/all_to_all | solution.py:174
  142.1 1.6 copy.12
  143.7 8.8 %fusion.15 = f32[48,1024]{1,0:T(8,128)S(1)} fusion(bf16[48,8192]{1,0:T(8,128)(2,1)S(1)} %bitcast.30, bf16[8192,1024]{1,0:T(8,128)(2,1)} %param.9), kind=kOutput, calls=%fused_computation.52 | convolution fusion | flops 805306368 | bytes 17760256 | tf_op jit(solution)/shard_map/dot_general | solution.py:177
  153.0 1.6 collective-permute-start.2
  154.8 14.1 %all-to-all-done.3 = bf16[16,5,32,256]{3,2,1,0:T(8,128)(2,1)S(1)} async-done(((bf16[16,5,32,256]{3,2,1,0:T(8,128)(2,1)}), bf16[16,5,32,256]{3,2,1,0:T(8,128)(2,1)S(1)}, u32[]{:S(2)}, u32[]{:S(2)}) %all-to-all-start.3) | async-done | bytes 1310752 | tf_op jit(solution)/shard_map/all_to_all | solution.py:174
  168.8 0.8 copy.13
  169.7 8.8 %fusion.16 = f32[80,1024]{1,0:T(8,128)S(1)} fusion(bf16[80,8192]{1,0:T(8,128)(2,1)S(1)} %bitcast.28, bf16[8192,1024]{1,0:T(8,128)(2,1)} %param.9), kind=kOutput, calls=%fused_computation.53 | convolution fusion | flops 1342177280 | bytes 18415616 | tf_op jit(solution)/shard_map/dot_general | solution.py:177
  178.5 0.8 collective-permute-start.9
  179.4 2.0 collective-permute-start.11
  181.8 4.5 %collective-permute-start.5 = (f32[48,256]{1,0:T(8,128)S(1)}, f32[48,256]{1,0:T(8,128)S(1)}, u32[]{:S(2)}, u32[]{:S(2)}) collective-permute-start(f32[48,256]{1,0:T(8,128)S(1)} %add_add_fusion.3), channel_id=1, source_target_pairs={{0,12},{1,13},{2,14},{3,15},{4,8},{5,9},{6,10},{7,11},{8,4},{9,5},... | collective-permute-start | bytes 147464 | tf_op jit(solution)/shard_map/ppermute | solution.py:112
  186.2 0.9 collective-permute-start.4
  187.7 3.1 %collective-permute-start.14 = (f32[80,256]{1,0:T(8,128)S(1)}, f32[80,256]{1,0:T(8,128)S(1)}, u32[]{:S(2)}, u32[]{:S(2)}) collective-permute-start(f32[80,256]{1,0:T(8,128)S(1)} %add_add_fusion.1), channel_id=1, source_target_pairs={{0,12},{1,13},{2,14},{3,15},{4,8},{5,9},{6,10},{7,11},{8,4},{9,5},... | collective-permute-start | bytes 245768 | tf_op jit(solution)/shard_map/ppermute | solution.py:112
  190.8 0.8 collective-permute-start.13
  192.4 2.2 collective-permute-start.7
  194.7 4.2 %collective-permute-done.13 = f32[80,256]{1,0:T(8,128)S(1)} collective-permute-done((f32[80,256]{1,0:T(8,128)S(1)}, f32[80,256]{1,0:T(8,128)S(1)}, u32[]{:S(2)}, u32[]{:S(2)}) %collective-permute-start.13) | collective-permute-done | bytes 81952 | tf_op jit(solution)/shard_map/ppermute | solution.py:112
  199.0 1.5 collective-permute-start.16
  200.9 3.3 %collective-permute-done.16 = f32[80,256]{1,0:T(8,128)S(1)} collective-permute-done((f32[80,256]{1,0:T(8,128)S(1)}, f32[80,256]{1,0:T(8,128)S(1)}, u32[]{:S(2)}, u32[]{:S(2)}) %collective-permute-start.16) | collective-permute-done | bytes 81952 | tf_op jit(solution)/shard_map/ppermute | solution.py:112
  204.2 1.1 collective-permute-done.15
  206.2 0.9 convert_reduce_fusion
  207.1 14.1 %fusion = f32[8192,1024]{1,0:T(8,128)} fusion(bf16[128,1024]{1,0:T(8,128)(2,1)S(1)} %get-tuple-element.8, bf16[80,8192]{1,0:T(8,128)(2,1)S(1)} %bitcast.29, bf16[48,8192]{1,0:T(8,128)(2,1)S(1)} %bitcast.31), kind=kOutput, calls=%fused_computation | convolution fusion | flops 2151677952 | bytes 35913728 | tf_op jit(solution)/shard_map/dot_general | solution.py:191
  (43 shorter events, 3.7 us)
Async XLA Ops:
  3.7 39.4 %all-to-all-start = ((bf16[16,3,32,512]{3,2,1,0:T(8,128)(2,1)}), bf16[16,3,32,512]{3,2,1,0:T(8,128)(2,1)S(1)}, u32[]{:S(2)}, u32[]{:S(2)}) async-start(bf16[16,3,32,512]{3,2,1,0:T(8,128)(2,1)} %bitcast.2), calls=%async_computation | async-start | bytes 3145728 | tf_op jit(solution)/shard_map/all_to_all | solution.py:168
  43.0 1.2 copy-start.1
  44.2 13.4 %copy-start = (bf16[1024,512]{1,0:T(8,128)(2,1)S(1)}, bf16[1024,512]{1,0:T(8,128)(2,1)}, u32[]{:S(2)}) copy-start(bf16[1024,512]{1,0:T(8,128)(2,1)} %constant.64.clone.table_ref) | copy-start | bytes 3145732
  44.2 59.6 %all-to-all-start.2 = ((bf16[16,5,32,512]{3,2,1,0:T(8,128)(2,1)}), bf16[16,5,32,512]{3,2,1,0:T(8,128)(2,1)}, u32[]{:S(2)}, u32[]{:S(2)}) async-start(bf16[16,5,32,512]{3,2,1,0:T(8,128)(2,1)} %bitcast.4), calls=%async_computation.2 | async-start | bytes 5242880 | tf_op jit(solution)/shard_map/all_to_all | solution.py:168
  103.8 32.1 %all-to-all-start.1 = ((bf16[16,3,32,256]{3,2,1,0:T(8,128)(2,1)}), bf16[16,3,32,256]{3,2,1,0:T(8,128)(2,1)}, u32[]{:S(2)}, u32[]{:S(2)}) async-start(bf16[16,3,32,256]{3,2,1,0:T(8,128)(2,1)} %spectrum.2), calls=%async_computation.1 | async-start | bytes 1572864 | tf_op jit(solution)/shard_map/all_to_all | solution.py:174
  135.9 32.9 %all-to-all-start.3 = ((bf16[16,5,32,256]{3,2,1,0:T(8,128)(2,1)}), bf16[16,5,32,256]{3,2,1,0:T(8,128)(2,1)S(1)}, u32[]{:S(2)}, u32[]{:S(2)}) async-start(bf16[16,5,32,256]{3,2,1,0:T(8,128)(2,1)} %spectrum.3), calls=%async_computation.3 | async-start | bytes 2621440 | tf_op jit(solution)/shard_map/all_to_all | solution.py:174
  152.5 28.8 %collective-permute-start = (f32[48,256]{1,0:T(8,128)S(1)}, f32[48,256]{1,0:T(8,128)S(1)}, u32[]{:S(2)}, u32[]{:S(2)}) collective-permute-start(f32[48,256]{1,0:T(8,128)S(1)} %get-tuple-element.23), channel_id=1, source_target_pairs={{0,1},{1,0},{2,3},{3,2},{4,5},{5,4},{6,7},{7,6},{8,9},{9,8},{10,11... | collective-permute-start | bytes 147464 | tf_op jit(solution)/shard_map/ppermute | solution.py:112
  153.0 28.8 %collective-permute-start.2 = (f32[48,256]{1,0:T(8,128)S(1)}, f32[48,256]{1,0:T(8,128)S(1)}, u32[]{:S(2)}, u32[]{:S(2)}) collective-permute-start(f32[48,256]{1,0:T(8,128)S(1)} %get-tuple-element.24), channel_id=1, source_target_pairs={{0,3},{1,2},{2,1},{3,0},{4,7},{5,6},{6,5},{7,4},{8,11},{9,10},{10,... | collective-permute-start | bytes 147464 | tf_op jit(solution)/shard_map/ppermute | solution.py:112
  154.6 27.1 %collective-permute-start.1 = (f32[48,256]{1,0:T(8,128)S(1)}, f32[48,256]{1,0:T(8,128)S(1)}, u32[]{:S(2)}, u32[]{:S(2)}) collective-permute-start(f32[48,256]{1,0:T(8,128)S(1)} %get-tuple-element.25), channel_id=1, source_target_pairs={{0,2},{1,3},{2,0},{3,1},{4,6},{5,7},{6,4},{7,5},{8,10},{9,11},{10,... | collective-permute-start | bytes 147464 | tf_op jit(solution)/shard_map/ppermute | solution.py:112
  178.5 26.8 %copy-start.2 = (f32[1024]{0:T(1024)S(1)}, f32[1024]{0:T(1024)}, u32[]{:S(2)}) copy-start(f32[1024]{0:T(1024)} %param.11) | copy-start | bytes 12292
  178.5 26.8 %copy-start.3 = (f32[1024]{0:T(1024)S(1)}, f32[1024]{0:T(1024)}, u32[]{:S(2)}) copy-start(f32[1024]{0:T(1024)} %param.10) | copy-start | bytes 12292
  178.5 27.1 %copy-start.4 = (s32[128]{0:T(128)S(1)}, s32[128]{0:T(128)}, u32[]{:S(2)}) copy-start(s32[128]{0:T(128)} %param.8) | copy-start | bytes 1540
  178.5 8.6 %collective-permute-start.9 = (f32[80,256]{1,0:T(8,128)S(1)}, f32[80,256]{1,0:T(8,128)S(1)}, u32[]{:S(2)}, u32[]{:S(2)}) collective-permute-start(f32[80,256]{1,0:T(8,128)S(1)} %get-tuple-element.16), channel_id=1, source_target_pairs={{0,1},{1,0},{2,3},{3,2},{4,5},{5,4},{6,7},{7,6},{8,9},{9,8},{10,11... | collective-permute-start | bytes 245768 | tf_op jit(solution)/shard_map/ppermute | solution.py:112
  179.4 8.3 %collective-permute-start.11 = (f32[80,256]{1,0:T(8,128)S(1)}, f32[80,256]{1,0:T(8,128)S(1)}, u32[]{:S(2)}, u32[]{:S(2)}) collective-permute-start(f32[80,256]{1,0:T(8,128)S(1)} %get-tuple-element.17), channel_id=1, source_target_pairs={{0,3},{1,2},{2,1},{3,0},{4,7},{5,6},{6,5},{7,4},{8,11},{9,10},{10,... | collective-permute-start | bytes 245768 | tf_op jit(solution)/shard_map/ppermute | solution.py:112
  181.4 6.3 %collective-permute-start.10 = (f32[80,256]{1,0:T(8,128)S(1)}, f32[80,256]{1,0:T(8,128)S(1)}, u32[]{:S(2)}, u32[]{:S(2)}) collective-permute-start(f32[80,256]{1,0:T(8,128)S(1)} %get-tuple-element.18), channel_id=1, source_target_pairs={{0,2},{1,3},{2,0},{3,1},{4,6},{5,7},{6,4},{7,5},{8,10},{9,11},{10,... | collective-permute-start | bytes 245768 | tf_op jit(solution)/shard_map/ppermute | solution.py:112
  181.8 9.8 %collective-permute-start.5 = (f32[48,256]{1,0:T(8,128)S(1)}, f32[48,256]{1,0:T(8,128)S(1)}, u32[]{:S(2)}, u32[]{:S(2)}) collective-permute-start(f32[48,256]{1,0:T(8,128)S(1)} %add_add_fusion.3), channel_id=1, source_target_pairs={{0,12},{1,13},{2,14},{3,15},{4,8},{5,9},{6,10},{7,11},{8,4},{9,5},... | collective-permute-start | bytes 147464 | tf_op jit(solution)/shard_map/ppermute | solution.py:112
  186.2 5.9 %collective-permute-start.4 = (f32[48,256]{1,0:T(8,128)S(1)}, f32[48,256]{1,0:T(8,128)S(1)}, u32[]{:S(2)}, u32[]{:S(2)}) collective-permute-start(f32[48,256]{1,0:T(8,128)S(1)} %add_add_fusion.3), channel_id=1, source_target_pairs={{0,8},{1,9},{2,10},{3,11},{4,12},{5,13},{6,14},{7,15},{8,0},{9,1},... | collective-permute-start | bytes 147464 | tf_op jit(solution)/shard_map/ppermute | solution.py:112
  187.2 5.1 %collective-permute-start.3 = (f32[48,256]{1,0:T(8,128)S(1)}, f32[48,256]{1,0:T(8,128)S(1)}, u32[]{:S(2)}, u32[]{:S(2)}) collective-permute-start(f32[48,256]{1,0:T(8,128)S(1)} %add_add_fusion.3), channel_id=1, source_target_pairs={{0,4},{1,5},{2,6},{3,7},{4,0},{5,1},{6,2},{7,3},{8,12},{9,13},{10,... | collective-permute-start | bytes 147464 | tf_op jit(solution)/shard_map/ppermute | solution.py:112
  187.7 6.9 %collective-permute-start.14 = (f32[80,256]{1,0:T(8,128)S(1)}, f32[80,256]{1,0:T(8,128)S(1)}, u32[]{:S(2)}, u32[]{:S(2)}) collective-permute-start(f32[80,256]{1,0:T(8,128)S(1)} %add_add_fusion.1), channel_id=1, source_target_pairs={{0,12},{1,13},{2,14},{3,15},{4,8},{5,9},{6,10},{7,11},{8,4},{9,5},... | collective-permute-start | bytes 245768 | tf_op jit(solution)/shard_map/ppermute | solution.py:112
  190.8 8.1 %collective-permute-start.13 = (f32[80,256]{1,0:T(8,128)S(1)}, f32[80,256]{1,0:T(8,128)S(1)}, u32[]{:S(2)}, u32[]{:S(2)}) collective-permute-start(f32[80,256]{1,0:T(8,128)S(1)} %add_add_fusion.1), channel_id=1, source_target_pairs={{0,8},{1,9},{2,10},{3,11},{4,12},{5,13},{6,14},{7,15},{8,0},{9,1},... | collective-permute-start | bytes 245768 | tf_op jit(solution)/shard_map/ppermute | solution.py:112
  191.6 7.3 %collective-permute-start.12 = (f32[80,256]{1,0:T(8,128)S(1)}, f32[80,256]{1,0:T(8,128)S(1)}, u32[]{:S(2)}, u32[]{:S(2)}) collective-permute-start(f32[80,256]{1,0:T(8,128)S(1)} %add_add_fusion.1), channel_id=1, source_target_pairs={{0,4},{1,5},{2,6},{3,7},{4,0},{5,1},{6,2},{7,3},{8,12},{9,13},{10,... | collective-permute-start | bytes 245768 | tf_op jit(solution)/shard_map/ppermute | solution.py:112
  192.3 8.3 %collective-permute-start.8 = (f32[48,256]{1,0:T(8,128)S(1)}, f32[48,256]{1,0:T(8,128)S(1)}, u32[]{:S(2)}, u32[]{:S(2)}) collective-permute-start(f32[48,256]{1,0:T(8,128)S(1)} %add_add_fusion.2), channel_id=1, source_target_pairs={{0,1},{1,0},{2,3},{3,2},{4,5},{5,4},{6,7},{7,6},{8,9},{9,8},{10,11... | collective-permute-start | bytes 147464 | tf_op jit(solution)/shard_map/ppermute | solution.py:112
  192.4 8.5 %collective-permute-start.7 = (f32[48,256]{1,0:T(8,128)S(1)}, f32[48,256]{1,0:T(8,128)S(1)}, u32[]{:S(2)}, u32[]{:S(2)}) collective-permute-start(f32[48,256]{1,0:T(8,128)S(1)} %add_add_fusion.2), channel_id=1, source_target_pairs={{0,2},{1,3},{2,0},{3,1},{4,6},{5,7},{6,4},{7,5},{8,10},{9,11},{10,... | collective-permute-start | bytes 147464 | tf_op jit(solution)/shard_map/ppermute | solution.py:112
  194.6 6.3 %collective-permute-start.6 = (f32[48,256]{1,0:T(8,128)S(1)}, f32[48,256]{1,0:T(8,128)S(1)}, u32[]{:S(2)}, u32[]{:S(2)}) collective-permute-start(f32[48,256]{1,0:T(8,128)S(1)} %add_add_fusion.2), channel_id=1, source_target_pairs={{0,3},{1,2},{2,1},{3,0},{4,7},{5,6},{6,5},{7,4},{8,11},{9,10},{10,... | collective-permute-start | bytes 147464 | tf_op jit(solution)/shard_map/ppermute | solution.py:112
  198.9 2.0 collective-permute-start.17
  199.0 5.2 %collective-permute-start.16 = (f32[80,256]{1,0:T(8,128)S(1)}, f32[80,256]{1,0:T(8,128)S(1)}, u32[]{:S(2)}, u32[]{:S(2)}) collective-permute-start(f32[80,256]{1,0:T(8,128)S(1)} %add_add_fusion), channel_id=1, source_target_pairs={{0,2},{1,3},{2,0},{3,1},{4,6},{5,7},{6,4},{7,5},{8,10},{9,11},{10,... | collective-permute-start | bytes 245768 | tf_op jit(solution)/shard_map/ppermute | solution.py:112
  200.6 4.7 %collective-permute-start.15 = (f32[80,256]{1,0:T(8,128)S(1)}, f32[80,256]{1,0:T(8,128)S(1)}, u32[]{:S(2)}, u32[]{:S(2)}) collective-permute-start(f32[80,256]{1,0:T(8,128)S(1)} %add_add_fusion), channel_id=1, source_target_pairs={{0,3},{1,2},{2,1},{3,0},{4,7},{5,6},{6,5},{7,4},{8,11},{9,10},{10,... | collective-permute-start | bytes 245768 | tf_op jit(solution)/shard_map/ppermute | solution.py:112

commit v3 on v2

--- a/solution.py
+++ b/solution.py
@@ -15,6 +15,7 @@
 LANES = 128
 ROW_BLOCK = 8
 VMEM_LIMIT = 50 * 2**20
+PRODUCT_STEP = 512
 
 
 def tables():
@@ -108,8 +109,92 @@
     )(blocks, *consts)
 
 
+def gradient_kernel(*refs, block, slots):
+    *feat_refs, dpre_ref, o_ref, buffer, sems = refs
+    blocks = o_ref.shape[0] // block
+
+    def copy(k):
+        return pltpu.make_async_copy(
+            buffer.at[k % slots], o_ref.at[pl.ds(k * block, block), :], sems.at[k % slots]
+        )
+
+    for k in range(blocks):
+        if k >= slots:
+            copy(k - slots).wait()
+        feats = jnp.concatenate([ref[:, k * block : (k + 1) * block] for ref in feat_refs], 0)
+        buffer[k % slots] = lax.dot_general(
+            feats, dpre_ref[...], (((0,), (0,)), ((), ())), preferred_element_type=jnp.float32
+        )
+        copy(k).start()
+    for k in range(max(0, blocks - slots), blocks):
+        copy(k).wait()
+
+
+def gradient(chunks, dpre):
+    features, hid = chunks[0].shape[1], dpre.shape[1]
+    block = min(256, features)
+    slots = min(8, features // block)
+    return pl.pallas_call(
+        functools.partial(gradient_kernel, block=block, slots=slots),
+        in_specs=[pl.BlockSpec(memory_space=pltpu.VMEM)] * (len(chunks) + 1),
+        out_specs=pl.BlockSpec(memory_space=pl.ANY),
+        out_shape=jax.ShapeDtypeStruct((features, hid), jnp.float32),
+        scratch_shapes=[
+            pltpu.VMEM((slots, block, hid), jnp.float32),
+            pltpu.SemaphoreType.DMA((slots,)),
+        ],
+        compiler_params=pltpu.CompilerParams(vmem_limit_bytes=24 * 2**20),
+        cost_estimate=pl.CostEstimate(
+            flops=2 * features * hid * dpre.shape[0],
+            bytes_accessed=features * hid * 4,
+            transcendentals=0,
+        ),
+        name="gradient",
+    )(*chunks, dpre)
+
+
 def exchange(value, bit, devices):
     return lax.ppermute(value, "tm", [(i, i ^ bit) for i in range(devices)])
+
+
+def product_kernel(feats_ref, weight_ref, o_ref, held_ref, sems, *, step):
+    copies = []
+    for k in range(weight_ref.shape[0] // step):
+        rows = pl.ds(k * step, step)
+        copies.append(
+            pltpu.make_async_copy(weight_ref.at[rows, :], held_ref.at[rows, :], sems.at[k])
+        )
+        copies[-1].start()
+    total = None
+    for k, copy in enumerate(copies):
+        copy.wait()
+        rows = slice(k * step, (k + 1) * step)
+        piece = jnp.dot(
+            feats_ref[:, rows], held_ref[rows, :], preferred_element_type=jnp.float32
+        )
+        total = piece if total is None else total + piece
+    o_ref[...] = total
+
+
+def product(feats, weight):
+    rows, (depth, hid) = feats.shape[0], weight.shape
+    step = min(PRODUCT_STEP, depth)
+    vmem = pl.BlockSpec(memory_space=pltpu.VMEM)
+    return pl.pallas_call(
+        functools.partial(product_kernel, step=step),
+        in_specs=[vmem, pl.BlockSpec(memory_space=pl.ANY)],
+        out_specs=vmem,
+        out_shape=jax.ShapeDtypeStruct((rows, hid), jnp.float32),
+        scratch_shapes=[
+            pltpu.VMEM((depth, hid), weight.dtype),
+            pltpu.SemaphoreType.DMA((depth // step,)),
+        ],
+        compiler_params=pltpu.CompilerParams(vmem_limit_bytes=49 * 2**20),
+        cost_estimate=pl.CostEstimate(
+            flops=2 * rows * weight.size, bytes_accessed=weight.size * 2, transcendentals=0
+        ),
+        name="product",
+    )(feats, weight)
 
 
 def sum_over(value, devices):
@@ -174,10 +259,9 @@
         feats = lax.all_to_all(feats, "tm", split_axis=0, concat_axis=0, tiled=True)
         feats = feats.reshape(rows, slow * HALF)
         feature_chunks.append(feats)
-        partial_sums = jnp.dot(feats, first_weight, preferred_element_type=jnp.float32)
+        partial_sums = product(feats, first_weight)
         pre_chunks.append(sum_over(partial_sums, devices))
         row += rows
-    features = jnp.concatenate(feature_chunks, 0)
     pre = jnp.concatenate(pre_chunks, 0) + first_bias[None, :]
 
     target = labels.astype(jnp.float32)
@@ -188,9 +272,7 @@
     dpre = (dlogit[:, None] * second_weight[None, :] * gate * (1.0 + pre * (1.0 - gate))).astype(
         jnp.bfloat16
     )
-    grad_first = lax.dot_general(
-        features, dpre, (((0,), (0,)), ((), ())), preferred_element_type=jnp.float32
-    )
+    grad_first = gradient(feature_chunks, dpre)
     grad_bias = jnp.sum(dpre.astype(jnp.float32), 0)
     grad_second = jnp.sum(hidden * dlogit[:, None], 0)
     loss = jnp.mean(jnp.log(1.0 + jnp.exp(logit)) - target * logit).reshape(1)

time: 224 us -> 218 us (0.973)
  matrix products: 31.7 us -> 0 us
  Pallas kernels: 26.1 us -> 49.9 us
  waiting for transfers between devices: 96.7 us -> 99.1 us
    dot_general x3 -> x0, matrix products: 31.7 us -> none  [the longest x2 17.6 us: on_device(): jnp.dot(feats, first_weight, preferred_element_type=jnp.float32)]
    pallas_call x0 -> x3, Pallas kernels: none -> 23.7 us  [the longest x2 12.5 us: product(): pl.pallas_call(functools.partial(product_kernel, step=step), in_specs=[vm...]
    all_to_all x2, waiting for transfers between devices: 21.4 us -> 23.8 us  [on_device(): feats = lax.all_to_all(feats, 'tm', split_axis=0, concat_axis=0, tiled=True)]
  transfers between devices with their start and end apart: 22 -> 22, of which waited for: 8 -> 8; matrix products, arithmetic and copies ran while one was open for 11% -> 3% of each run, Pallas kernels for 10% -> 16%
where the time goes in v3:
time: 218 us; the launch traced here: 217 us
  waiting for transfers between devices  99.1 us (45%)
  starting transfers between devices  55.6 us (26%)
  Pallas kernels  49.9 us (23%)
  other arithmetic  5.97 us (3%)
  local copies, waits for them, and re-layouts  3.63 us (2%)
  between operations  3.28 us (2%)
    all_to_all x2, waiting for transfers between devices, on_device(): blocks = lax.all_to_all(mine, 'tm', split_axis=0, concat_axis=0, tiled=True)  66.5 us
    all_to_all x2, waiting for transfers between devices, on_device(): feats = lax.all_to_all(feats, 'tm', split_axis=0, concat_axis=0, tiled=True)  23.8 us
    ppermute x18, starting transfers between devices, exchange(): return lax.ppermute(value, 'tm', [(i, i ^ bit) for i in range(devices)])  20 us
    pallas_call x2, Pallas kernels, spectrum(): pl.pallas_call(functools.partial(spectrum_kernel, block=max(128, slow)),...  19.1 us
    all_to_all x2, starting transfers between devices, on_device(): feats = lax.all_to_all(feats, 'tm', split_axis=0, concat_axis=0, tiled=True)  19 us
    all_to_all x2, starting transfers between devices, on_device(): blocks = lax.all_to_all(mine, 'tm', split_axis=0, concat_axis=0, tiled=True)  16.5 us
    pallas_call x2, Pallas kernels, product(): pl.pallas_call(functools.partial(product_kernel, step=step), in_specs=[vm...  12.5 us
    pallas_call x1, Pallas kernels, gradient(): pl.pallas_call(functools.partial(gradient_kernel, block=block, slots=slot...  11.3 us
  transfers between devices with their start and end apart: 22, of which 8 were waited for; matrix products, arithmetic and copies ran while one was open for 3% of the time, Pallas kernels for 16%

profile of v3, /device:TPU:0, one launch (start us, length us, event | category | flops | bytes accessed | tf_op | source)
XLA Modules:
  0.0 217.4 jit_solution(11531552516342131862)
XLA Ops:
  0.6 3.0 %prepare.2 = bf16[48,32,512]{2,1,0:T(8,128)(2,1)} custom-call(f32[16,32,4,8,128]{4,3,2,1,0:T(8,128)} %bitcast.19, f32[16,32,4,8,128]{4,3,2,1,0:T(8,128)} %bitcast.20, f32[16,32,4,8,128]{4,3,2,1,0:T(8,128)} %bitcast.21), custom_call_target="tpu_custom_call" | custom-call | flops 786432 | bytes 4718592 | tf_op jit(solution)/shard_map/prepare/pallas_call | solution.py:53
  3.7 7.4 %all-to-all-start = ((bf16[16,3,32,512]{3,2,1,0:T(8,128)(2,1)}), bf16[16,3,32,512]{3,2,1,0:T(8,128)(2,1)S(1)}, u32[]{:S(2)}, u32[]{:S(2)}) async-start(bf16[16,3,32,512]{3,2,1,0:T(8,128)(2,1)} %bitcast.2), calls=%async_computation | async-start | bytes 3145728 | tf_op jit(solution)/shard_map/all_to_all | solution.py:253
  11.1 4.0 %prepare.3 = bf16[80,32,512]{2,1,0:T(8,128)(2,1)} custom-call(f32[16,32,4,8,128]{4,3,2,1,0:T(8,128)} %bitcast.22, f32[16,32,4,8,128]{4,3,2,1,0:T(8,128)} %bitcast.23, f32[16,32,4,8,128]{4,3,2,1,0:T(8,128)} %bitcast.24, f32[16,32,4,8,128]{4,3,2,1,0:T(8,128)} %bitcast.25, f32[16,32,4,8,128]{4,3,2,1,0:T(8,128)} %bitcast.26), custom_call_target="tpu_custom_call" | custom-call | flops 1310720 | bytes 7864320 | tf_op jit(solution)/shard_map/prepare/pallas_call | solution.py:53
  15.1 28.0 %all-to-all-done.x_ref = bf16[16,3,32,512]{3,2,1,0:T(8,128)(2,1)S(1)} async-done(((bf16[16,3,32,512]{3,2,1,0:T(8,128)(2,1)}), bf16[16,3,32,512]{3,2,1,0:T(8,128)(2,1)S(1)}, u32[]{:S(2)}, u32[]{:S(2)}) %all-to-all-start) | async-done | bytes 1572896 | tf_op jit(solution)/shard_map/all_to_all | solution.py:253
  43.1 1.1 copy-done.1
  44.2 9.2 %all-to-all-start.2 = ((bf16[16,5,32,512]{3,2,1,0:T(8,128)(2,1)}), bf16[16,5,32,512]{3,2,1,0:T(8,128)(2,1)}, u32[]{:S(2)}, u32[]{:S(2)}) async-start(bf16[16,5,32,512]{3,2,1,0:T(8,128)(2,1)} %bitcast.4), calls=%async_computation.2 | async-start | bytes 5242880 | tf_op jit(solution)/shard_map/all_to_all | solution.py:253
  53.4 4.1 %fusion.7 = (f32[512,512]{1,0:T(8,128)S(1)}, f32[512,512]{1,0:T(8,128)S(1)}) fusion(), kind=kLoop, calls=%fused_computation.16 | loop fusion | flops 3670016 | bytes 2097152 | tf_op jit(solution)/shard_map/sin | solution.py:31
  57.5 7.6 %spectrum.2 = bf16[16,3,32,256]{3,2,1,0:T(8,128)(2,1)} custom-call(bf16[16,3,32,512]{3,2,1,0:T(8,128)(2,1)} %copy-done.1, bf16[1024,512]{1,0:T(8,128)(2,1)S(1)} %copy-done, f32[512,512]{1,0:T(8,128)S(1)} %get-tuple-element.28.cos_ref, f32[512,512]{1,0:T(8,128)S(1)} %get-tuple-element.27.sin_ref), custom_call_target="tpu_custom_call" | custom-call | flops 3221225472 | bytes 6553600 | tf_op jit(solution)/shard_map/spectrum/pallas_call | solution.py:95
  65.1 38.6 %all-to-all-done.2.x_ref = bf16[16,5,32,512]{3,2,1,0:T(8,128)(2,1)} async-done(((bf16[16,5,32,512]{3,2,1,0:T(8,128)(2,1)}), bf16[16,5,32,512]{3,2,1,0:T(8,128)(2,1)}, u32[]{:S(2)}, u32[]{:S(2)}) %all-to-all-start.2) | async-done | bytes 2621472 | tf_op jit(solution)/shard_map/all_to_all | solution.py:253
  103.7 13.4 %all-to-all-start.1 = ((bf16[16,3,32,256]{3,2,1,0:T(8,128)(2,1)}), bf16[16,3,32,256]{3,2,1,0:T(8,128)(2,1)}, u32[]{:S(2)}, u32[]{:S(2)}) async-start(bf16[16,3,32,256]{3,2,1,0:T(8,128)(2,1)} %spectrum.2), calls=%async_computation.1 | async-start | bytes 1572864 | tf_op jit(solution)/shard_map/all_to_all | solution.py:259
  117.0 11.5 %spectrum.3 = bf16[16,5,32,256]{3,2,1,0:T(8,128)(2,1)} custom-call(bf16[16,5,32,512]{3,2,1,0:T(8,128)(2,1)} %all-to-all-done.2.x_ref, bf16[1024,512]{1,0:T(8,128)(2,1)S(1)} %copy-done, f32[512,512]{1,0:T(8,128)S(1)} %get-tuple-element.28.cos_ref, f32[512,512]{1,0:T(8,128)S(1)} %get-tuple-element.27.sin_ref), custom_call_target="tpu_custom_call" | custom-call | flops 5368709120 | bytes 8126464 | tf_op jit(solution)/shard_map/spectrum/pallas_call | solution.py:95
  128.5 7.3 %all-to-all-done.1 = bf16[16,3,32,256]{3,2,1,0:T(8,128)(2,1)} async-done(((bf16[16,3,32,256]{3,2,1,0:T(8,128)(2,1)}), bf16[16,3,32,256]{3,2,1,0:T(8,128)(2,1)}, u32[]{:S(2)}, u32[]{:S(2)}) %all-to-all-start.1) | async-done | bytes 786464 | tf_op jit(solution)/shard_map/all_to_all | solution.py:259
  135.8 5.7 %all-to-all-start.3 = ((bf16[16,5,32,256]{3,2,1,0:T(8,128)(2,1)}), bf16[16,5,32,256]{3,2,1,0:T(8,128)(2,1)S(1)}, u32[]{:S(2)}, u32[]{:S(2)}) async-start(bf16[16,5,32,256]{3,2,1,0:T(8,128)(2,1)} %spectrum.3), calls=%async_computation.3 | async-start | bytes 2621440 | tf_op jit(solution)/shard_map/all_to_all | solution.py:259
  142.2 1.6 copy.12
  143.8 6.2 %product.2 = f32[48,1024]{1,0:T(8,128)S(1)} custom-call(bf16[48,8192]{1,0:T(8,128)(2,1)S(1)} %bitcast.17, bf16[8192,1024]{1,0:T(8,128)(2,1)} %weight_ref.3), custom_call_target="tpu_custom_call" | custom-call | flops 805306368 | bytes 16777216 | tf_op jit(solution)/shard_map/product/pallas_call | solution.py:183
  150.3 1.6 collective-permute-start.2
  152.2 16.5 %all-to-all-done.3 = bf16[16,5,32,256]{3,2,1,0:T(8,128)(2,1)S(1)} async-done(((bf16[16,5,32,256]{3,2,1,0:T(8,128)(2,1)}), bf16[16,5,32,256]{3,2,1,0:T(8,128)(2,1)S(1)}, u32[]{:S(2)}, u32[]{:S(2)}) %all-to-all-start.3) | async-done | bytes 1310752 | tf_op jit(solution)/shard_map/all_to_all | solution.py:259
  168.7 0.8 copy.13
  169.5 6.2 %product.3 = f32[80,1024]{1,0:T(8,128)S(1)} custom-call(bf16[80,8192]{1,0:T(8,128)(2,1)S(1)} %bitcast.15, bf16[8192,1024]{1,0:T(8,128)(2,1)} %weight_ref.3), custom_call_target="tpu_custom_call" | custom-call | flops 1342177280 | bytes 16777216 | tf_op jit(solution)/shard_map/product/pallas_call | solution.py:183
  175.8 0.8 collective-permute-start.9
  176.7 2.0 collective-permute-start.11
  179.0 4.5 %collective-permute-start.5 = (f32[48,256]{1,0:T(8,128)S(1)}, f32[48,256]{1,0:T(8,128)S(1)}, u32[]{:S(2)}, u32[]{:S(2)}) collective-permute-start(f32[48,256]{1,0:T(8,128)S(1)} %add_add_fusion.3), channel_id=1, source_target_pairs={{0,12},{1,13},{2,14},{3,15},{4,8},{5,9},{6,10},{7,11},{8,4},{9,5},... | collective-permute-start | bytes 147464 | tf_op jit(solution)/shard_map/ppermute | solution.py:157
  183.5 0.9 collective-permute-start.4
  185.0 3.1 %collective-permute-start.14 = (f32[80,256]{1,0:T(8,128)S(1)}, f32[80,256]{1,0:T(8,128)S(1)}, u32[]{:S(2)}, u32[]{:S(2)}) collective-permute-start(f32[80,256]{1,0:T(8,128)S(1)} %add_add_fusion.1), channel_id=1, source_target_pairs={{0,12},{1,13},{2,14},{3,15},{4,8},{5,9},{6,10},{7,11},{8,4},{9,5},... | collective-permute-start | bytes 245768 | tf_op jit(solution)/shard_map/ppermute | solution.py:157
  188.1 0.8 collective-permute-start.13
  189.7 2.2 %collective-permute-start.7 = (f32[48,256]{1,0:T(8,128)S(1)}, f32[48,256]{1,0:T(8,128)S(1)}, u32[]{:S(2)}, u32[]{:S(2)}) collective-permute-start(f32[48,256]{1,0:T(8,128)S(1)} %add_add_fusion.2), channel_id=1, source_target_pairs={{0,2},{1,3},{2,0},{3,1},{4,6},{5,7},{6,4},{7,5},{8,10},{9,11},{10,... | collective-permute-start | bytes 147464 | tf_op jit(solution)/shard_map/ppermute | solution.py:157
  191.9 4.2 %collective-permute-done.13 = f32[80,256]{1,0:T(8,128)S(1)} collective-permute-done((f32[80,256]{1,0:T(8,128)S(1)}, f32[80,256]{1,0:T(8,128)S(1)}, u32[]{:S(2)}, u32[]{:S(2)}) %collective-permute-start.13) | collective-permute-done | bytes 81952 | tf_op jit(solution)/shard_map/ppermute | solution.py:157
  196.3 1.5 collective-permute-start.16
  198.2 3.3 %collective-permute-done.16 = f32[80,256]{1,0:T(8,128)S(1)} collective-permute-done((f32[80,256]{1,0:T(8,128)S(1)}, f32[80,256]{1,0:T(8,128)S(1)}, u32[]{:S(2)}, u32[]{:S(2)}) %collective-permute-start.16) | collective-permute-done | bytes 81952 | tf_op jit(solution)/shard_map/ppermute | solution.py:157
  201.5 1.1 collective-permute-done.15
  203.5 0.9 convert_reduce_fusion
  204.4 11.3 %gradient.1 = f32[8192,1024]{1,0:T(8,128)} custom-call(bf16[48,8192]{1,0:T(8,128)(2,1)S(1)} %bitcast.18, bf16[80,8192]{1,0:T(8,128)(2,1)S(1)} %bitcast.16, bf16[128,1024]{1,0:T(8,128)(2,1)S(1)} %get-tuple-element.8.refs_2_), custom_call_target="tpu_custom_call" | custom-call | flops 2147483648 | bytes 33554432 | tf_op jit(solution)/shard_map/gradient/pallas_call | solution.py:137
  (43 shorter events, 3.7 us)
Async XLA Ops:
  3.7 39.4 %all-to-all-start = ((bf16[16,3,32,512]{3,2,1,0:T(8,128)(2,1)}), bf16[16,3,32,512]{3,2,1,0:T(8,128)(2,1)S(1)}, u32[]{:S(2)}, u32[]{:S(2)}) async-start(bf16[16,3,32,512]{3,2,1,0:T(8,128)(2,1)} %bitcast.2), calls=%async_computation | async-start | bytes 3145728 | tf_op jit(solution)/shard_map/all_to_all | solution.py:253
  43.0 1.2 copy-start.1
  43.1 14.4 %copy-start = (bf16[1024,512]{1,0:T(8,128)(2,1)S(1)}, bf16[1024,512]{1,0:T(8,128)(2,1)}, u32[]{:S(2)}) copy-start(bf16[1024,512]{1,0:T(8,128)(2,1)} %constant.64.clone.table_ref) | copy-start | bytes 3145732
  44.2 59.5 %all-to-all-start.2 = ((bf16[16,5,32,512]{3,2,1,0:T(8,128)(2,1)}), bf16[16,5,32,512]{3,2,1,0:T(8,128)(2,1)}, u32[]{:S(2)}, u32[]{:S(2)}) async-start(bf16[16,5,32,512]{3,2,1,0:T(8,128)(2,1)} %bitcast.4), calls=%async_computation.2 | async-start | bytes 5242880 | tf_op jit(solution)/shard_map/all_to_all | solution.py:253
  103.7 32.1 %all-to-all-start.1 = ((bf16[16,3,32,256]{3,2,1,0:T(8,128)(2,1)}), bf16[16,3,32,256]{3,2,1,0:T(8,128)(2,1)}, u32[]{:S(2)}, u32[]{:S(2)}) async-start(bf16[16,3,32,256]{3,2,1,0:T(8,128)(2,1)} %spectrum.2), calls=%async_computation.1 | async-start | bytes 1572864 | tf_op jit(solution)/shard_map/all_to_all | solution.py:259
  135.8 32.9 %all-to-all-start.3 = ((bf16[16,5,32,256]{3,2,1,0:T(8,128)(2,1)}), bf16[16,5,32,256]{3,2,1,0:T(8,128)(2,1)S(1)}, u32[]{:S(2)}, u32[]{:S(2)}) async-start(bf16[16,5,32,256]{3,2,1,0:T(8,128)(2,1)} %spectrum.3), calls=%async_computation.3 | async-start | bytes 2621440 | tf_op jit(solution)/shard_map/all_to_all | solution.py:259
  150.0 28.7 %collective-permute-start = (f32[48,256]{1,0:T(8,128)S(1)}, f32[48,256]{1,0:T(8,128)S(1)}, u32[]{:S(2)}, u32[]{:S(2)}) collective-permute-start(f32[48,256]{1,0:T(8,128)S(1)} %get-tuple-element.23), channel_id=1, source_target_pairs={{0,1},{1,0},{2,3},{3,2},{4,5},{5,4},{6,7},{7,6},{8,9},{9,8},{10,11... | collective-permute-start | bytes 147464 | tf_op jit(solution)/shard_map/ppermute | solution.py:157
  150.3 28.7 %collective-permute-start.2 = (f32[48,256]{1,0:T(8,128)S(1)}, f32[48,256]{1,0:T(8,128)S(1)}, u32[]{:S(2)}, u32[]{:S(2)}) collective-permute-start(f32[48,256]{1,0:T(8,128)S(1)} %get-tuple-element.24), channel_id=1, source_target_pairs={{0,3},{1,2},{2,1},{3,0},{4,7},{5,6},{6,5},{7,4},{8,11},{9,10},{10,... | collective-permute-start | bytes 147464 | tf_op jit(solution)/shard_map/ppermute | solution.py:157
  151.9 27.1 %collective-permute-start.1 = (f32[48,256]{1,0:T(8,128)S(1)}, f32[48,256]{1,0:T(8,128)S(1)}, u32[]{:S(2)}, u32[]{:S(2)}) collective-permute-start(f32[48,256]{1,0:T(8,128)S(1)} %get-tuple-element.25), channel_id=1, source_target_pairs={{0,2},{1,3},{2,0},{3,1},{4,6},{5,7},{6,4},{7,5},{8,10},{9,11},{10,... | collective-permute-start | bytes 147464 | tf_op jit(solution)/shard_map/ppermute | solution.py:157
  175.8 26.8 %copy-start.2 = (f32[1024]{0:T(1024)S(1)}, f32[1024]{0:T(1024)}, u32[]{:S(2)}) copy-start(f32[1024]{0:T(1024)} %param.11) | copy-start | bytes 12292
  175.8 26.8 %copy-start.3 = (f32[1024]{0:T(1024)S(1)}, f32[1024]{0:T(1024)}, u32[]{:S(2)}) copy-start(f32[1024]{0:T(1024)} %param.10) | copy-start | bytes 12292
  175.8 27.1 %copy-start.4 = (s32[128]{0:T(128)S(1)}, s32[128]{0:T(128)}, u32[]{:S(2)}) copy-start(s32[128]{0:T(128)} %param.8) | copy-start | bytes 1540
  175.8 8.6 %collective-permute-start.9 = (f32[80,256]{1,0:T(8,128)S(1)}, f32[80,256]{1,0:T(8,128)S(1)}, u32[]{:S(2)}, u32[]{:S(2)}) collective-permute-start(f32[80,256]{1,0:T(8,128)S(1)} %get-tuple-element.16), channel_id=1, source_target_pairs={{0,1},{1,0},{2,3},{3,2},{4,5},{5,4},{6,7},{7,6},{8,9},{9,8},{10,11... | collective-permute-start | bytes 245768 | tf_op jit(solution)/shard_map/ppermute | solution.py:157
  176.7 8.3 %collective-permute-start.11 = (f32[80,256]{1,0:T(8,128)S(1)}, f32[80,256]{1,0:T(8,128)S(1)}, u32[]{:S(2)}, u32[]{:S(2)}) collective-permute-start(f32[80,256]{1,0:T(8,128)S(1)} %get-tuple-element.17), channel_id=1, source_target_pairs={{0,3},{1,2},{2,1},{3,0},{4,7},{5,6},{6,5},{7,4},{8,11},{9,10},{10,... | collective-permute-start | bytes 245768 | tf_op jit(solution)/shard_map/ppermute | solution.py:157
  178.7 6.3 %collective-permute-start.10 = (f32[80,256]{1,0:T(8,128)S(1)}, f32[80,256]{1,0:T(8,128)S(1)}, u32[]{:S(2)}, u32[]{:S(2)}) collective-permute-start(f32[80,256]{1,0:T(8,128)S(1)} %get-tuple-element.18), channel_id=1, source_target_pairs={{0,2},{1,3},{2,0},{3,1},{4,6},{5,7},{6,4},{7,5},{8,10},{9,11},{10,... | collective-permute-start | bytes 245768 | tf_op jit(solution)/shard_map/ppermute | solution.py:157
  179.0 9.8 %collective-permute-start.5 = (f32[48,256]{1,0:T(8,128)S(1)}, f32[48,256]{1,0:T(8,128)S(1)}, u32[]{:S(2)}, u32[]{:S(2)}) collective-permute-start(f32[48,256]{1,0:T(8,128)S(1)} %add_add_fusion.3), channel_id=1, source_target_pairs={{0,12},{1,13},{2,14},{3,15},{4,8},{5,9},{6,10},{7,11},{8,4},{9,5},... | collective-permute-start | bytes 147464 | tf_op jit(solution)/shard_map/ppermute | solution.py:157
  183.5 5.9 %collective-permute-start.4 = (f32[48,256]{1,0:T(8,128)S(1)}, f32[48,256]{1,0:T(8,128)S(1)}, u32[]{:S(2)}, u32[]{:S(2)}) collective-permute-start(f32[48,256]{1,0:T(8,128)S(1)} %add_add_fusion.3), channel_id=1, source_target_pairs={{0,8},{1,9},{2,10},{3,11},{4,12},{5,13},{6,14},{7,15},{8,0},{9,1},... | collective-permute-start | bytes 147464 | tf_op jit(solution)/shard_map/ppermute | solution.py:157
  184.4 5.1 %collective-permute-start.3 = (f32[48,256]{1,0:T(8,128)S(1)}, f32[48,256]{1,0:T(8,128)S(1)}, u32[]{:S(2)}, u32[]{:S(2)}) collective-permute-start(f32[48,256]{1,0:T(8,128)S(1)} %add_add_fusion.3), channel_id=1, source_target_pairs={{0,4},{1,5},{2,6},{3,7},{4,0},{5,1},{6,2},{7,3},{8,12},{9,13},{10,... | collective-permute-start | bytes 147464 | tf_op jit(solution)/shard_map/ppermute | solution.py:157
  185.0 6.9 %collective-permute-start.14 = (f32[80,256]{1,0:T(8,128)S(1)}, f32[80,256]{1,0:T(8,128)S(1)}, u32[]{:S(2)}, u32[]{:S(2)}) collective-permute-start(f32[80,256]{1,0:T(8,128)S(1)} %add_add_fusion.1), channel_id=1, source_target_pairs={{0,12},{1,13},{2,14},{3,15},{4,8},{5,9},{6,10},{7,11},{8,4},{9,5},... | collective-permute-start | bytes 245768 | tf_op jit(solution)/shard_map/ppermute | solution.py:157
  188.1 8.1 %collective-permute-start.13 = (f32[80,256]{1,0:T(8,128)S(1)}, f32[80,256]{1,0:T(8,128)S(1)}, u32[]{:S(2)}, u32[]{:S(2)}) collective-permute-start(f32[80,256]{1,0:T(8,128)S(1)} %add_add_fusion.1), channel_id=1, source_target_pairs={{0,8},{1,9},{2,10},{3,11},{4,12},{5,13},{6,14},{7,15},{8,0},{9,1},... | collective-permute-start | bytes 245768 | tf_op jit(solution)/shard_map/ppermute | solution.py:157
  188.9 7.3 %collective-permute-start.12 = (f32[80,256]{1,0:T(8,128)S(1)}, f32[80,256]{1,0:T(8,128)S(1)}, u32[]{:S(2)}, u32[]{:S(2)}) collective-permute-start(f32[80,256]{1,0:T(8,128)S(1)} %add_add_fusion.1), channel_id=1, source_target_pairs={{0,4},{1,5},{2,6},{3,7},{4,0},{5,1},{6,2},{7,3},{8,12},{9,13},{10,... | collective-permute-start | bytes 245768 | tf_op jit(solution)/shard_map/ppermute | solution.py:157
  189.6 8.3 %collective-permute-start.8 = (f32[48,256]{1,0:T(8,128)S(1)}, f32[48,256]{1,0:T(8,128)S(1)}, u32[]{:S(2)}, u32[]{:S(2)}) collective-permute-start(f32[48,256]{1,0:T(8,128)S(1)} %add_add_fusion.2), channel_id=1, source_target_pairs={{0,1},{1,0},{2,3},{3,2},{4,5},{5,4},{6,7},{7,6},{8,9},{9,8},{10,11... | collective-permute-start | bytes 147464 | tf_op jit(solution)/shard_map/ppermute | solution.py:157
  189.7 8.5 %collective-permute-start.7 = (f32[48,256]{1,0:T(8,128)S(1)}, f32[48,256]{1,0:T(8,128)S(1)}, u32[]{:S(2)}, u32[]{:S(2)}) collective-permute-start(f32[48,256]{1,0:T(8,128)S(1)} %add_add_fusion.2), channel_id=1, source_target_pairs={{0,2},{1,3},{2,0},{3,1},{4,6},{5,7},{6,4},{7,5},{8,10},{9,11},{10,... | collective-permute-start | bytes 147464 | tf_op jit(solution)/shard_map/ppermute | solution.py:157
  191.9 6.3 %collective-permute-start.6 = (f32[48,256]{1,0:T(8,128)S(1)}, f32[48,256]{1,0:T(8,128)S(1)}, u32[]{:S(2)}, u32[]{:S(2)}) collective-permute-start(f32[48,256]{1,0:T(8,128)S(1)} %add_add_fusion.2), channel_id=1, source_target_pairs={{0,3},{1,2},{2,1},{3,0},{4,7},{5,6},{6,5},{7,4},{8,11},{9,10},{10,... | collective-permute-start | bytes 147464 | tf_op jit(solution)/shard_map/ppermute | solution.py:157
  196.2 2.0 collective-permute-start.17
  196.3 5.2 %collective-permute-start.16 = (f32[80,256]{1,0:T(8,128)S(1)}, f32[80,256]{1,0:T(8,128)S(1)}, u32[]{:S(2)}, u32[]{:S(2)}) collective-permute-start(f32[80,256]{1,0:T(8,128)S(1)} %add_add_fusion), channel_id=1, source_target_pairs={{0,2},{1,3},{2,0},{3,1},{4,6},{5,7},{6,4},{7,5},{8,10},{9,11},{10,... | collective-permute-start | bytes 245768 | tf_op jit(solution)/shard_map/ppermute | solution.py:157
  197.8 4.7 %collective-permute-start.15 = (f32[80,256]{1,0:T(8,128)S(1)}, f32[80,256]{1,0:T(8,128)S(1)}, u32[]{:S(2)}, u32[]{:S(2)}) collective-permute-start(f32[80,256]{1,0:T(8,128)S(1)} %add_add_fusion), channel_id=1, source_target_pairs={{0,3},{1,2},{2,1},{3,0},{4,7},{5,6},{6,5},{7,4},{8,11},{9,10},{10,... | collective-permute-start | bytes 245768 | tf_op jit(solution)/shard_map/ppermute | solution.py:157

commit v4 on v3

--- a/solution.py
+++ b/solution.py
@@ -143,7 +143,7 @@
             pltpu.VMEM((slots, block, hid), jnp.float32),
             pltpu.SemaphoreType.DMA((slots,)),
         ],
-        compiler_params=pltpu.CompilerParams(vmem_limit_bytes=24 * 2**20),
+        compiler_params=pltpu.CompilerParams(vmem_limit_bytes=12 * 2**20),
         cost_estimate=pl.CostEstimate(
             flops=2 * features * hid * dpre.shape[0],
             bytes_accessed=features * hid * 4,
@@ -157,21 +157,33 @@
     return lax.ppermute(value, "tm", [(i, i ^ bit) for i in range(devices)])
 
 
-def product_kernel(feats_ref, weight_ref, o_ref, held_ref, sems, *, step):
+def product_kernel(feats_ref, weight_ref, o_ref, flat_ref, held_ref, sems, *, step):
     copies = []
     for k in range(weight_ref.shape[0] // step):
-        rows = pl.ds(k * step, step)
+        span = pl.ds(k * step, step)
         copies.append(
-            pltpu.make_async_copy(weight_ref.at[rows, :], held_ref.at[rows, :], sems.at[k])
+            pltpu.make_async_copy(weight_ref.at[span, :], held_ref.at[span, :], sems.at[k])
         )
         copies[-1].start()
+    if len(feats_ref.shape) == 3:
+        rows, slow, width = feats_ref.shape
+        for first in range(0, slow, 16):
+            for start in range(0, rows, 16):
+                for lane in range(0, width, LANES):
+                    value = feats_ref[
+                        start : start + 16, first : first + 16, lane : lane + LANES
+                    ]
+                    value = jnp.swapaxes(value, 0, 1)
+                    for k in range(16):
+                        column = (first + k) * width + lane
+                        flat_ref[start : start + 16, column : column + LANES] = value[k]
+    else:
+        flat_ref[...] = feats_ref[...]
     total = None
     for k, copy in enumerate(copies):
         copy.wait()
-        rows = slice(k * step, (k + 1) * step)
-        piece = jnp.dot(
-            feats_ref[:, rows], held_ref[rows, :], preferred_element_type=jnp.float32
-        )
+        span = slice(k * step, (k + 1) * step)
+        piece = jnp.dot(flat_ref[:, span], held_ref[span, :], preferred_element_type=jnp.float32)
         total = piece if total is None else total + piece
     o_ref[...] = total
 
@@ -183,8 +195,11 @@
     return pl.pallas_call(
         functools.partial(product_kernel, step=step),
         in_specs=[vmem, pl.BlockSpec(memory_space=pl.ANY)],
-        out_specs=vmem,
-        out_shape=jax.ShapeDtypeStruct((rows, hid), jnp.float32),
+        out_specs=[vmem, vmem],
+        out_shape=[
+            jax.ShapeDtypeStruct((rows, hid), jnp.float32),
+            jax.ShapeDtypeStruct((rows, depth), feats.dtype),
+        ],
         scratch_shapes=[
             pltpu.VMEM((depth, hid), weight.dtype),
             pltpu.SemaphoreType.DMA((depth // step,)),
@@ -249,6 +264,8 @@
     row = 0
     for size in chunks:
         rows = size * devices
+        if feature_chunks:
+            view, *consts = lax.optimization_barrier((view, *consts))
         mine = prepare(view, row, rows, slow).reshape(devices, size, slow, N1)
         blocks = lax.all_to_all(mine, "tm", split_axis=0, concat_axis=0, tiled=True)
         if not aligned:
@@ -257,9 +274,9 @@
         if not aligned:
             feats = feats.reshape(size, devices, slow, HALF).transpose(1, 0, 2, 3)
         feats = lax.all_to_all(feats, "tm", split_axis=0, concat_axis=0, tiled=True)
-        feats = feats.reshape(rows, slow * HALF)
+        feats = feats.reshape((rows, slow, HALF) if aligned else (rows, slow * HALF))
+        partial_sums, feats = product(feats, first_weight)
         feature_chunks.append(feats)
-        partial_sums = product(feats, first_weight)
         pre_chunks.append(sum_over(partial_sums, devices))
         row += rows
     pre = jnp.concatenate(pre_chunks, 0) + first_bias[None, :]

time: 218 us -> 217 us (level)
  transfers between devices with their start and end apart: 22 -> 22, of which waited for: 8 -> 9; matrix products, arithmetic and copies ran while one was open for 3% -> 2% of each run, Pallas kernels for 16% -> 16%
where the time goes in v4:
time: 217 us
  waiting for transfers between devices  97.5 us (45%)
  starting transfers between devices  55.9 us (26%)
  Pallas kernels  49.1 us (23%)
  other arithmetic  7.53 us (3%)
  local copies, waits for them, and re-layouts  3.41 us (2%)
  between operations  3.34 us (2%)
    all_to_all x2, waiting for transfers between devices, on_device(): blocks = lax.all_to_all(mine, 'tm', split_axis=0, concat_axis=0, tiled=True)  65.2 us
    all_to_all x2, waiting for transfers between devices, on_device(): feats = lax.all_to_all(feats, 'tm', split_axis=0, concat_axis=0, tiled=True)  24.1 us
    ppermute x18, starting transfers between devices, exchange(): return lax.ppermute(value, 'tm', [(i, i ^ bit) for i in range(devices)])  20.4 us
    all_to_all x2, starting transfers between devices, on_device(): feats = lax.all_to_all(feats, 'tm', split_axis=0, concat_axis=0, tiled=True)  19 us
    pallas_call x2, Pallas kernels, spectrum(): pl.pallas_call(functools.partial(spectrum_kernel, block=max(128, slow)),...  18.3 us
    all_to_all x2, starting transfers between devices, on_device(): blocks = lax.all_to_all(mine, 'tm', split_axis=0, concat_axis=0, tiled=True)  16.6 us
    pallas_call x2, Pallas kernels, product(): pl.pallas_call(functools.partial(product_kernel, step=step), in_specs=[vm...  12.5 us
    pallas_call x1, Pallas kernels, gradient(): pl.pallas_call(functools.partial(gradient_kernel, block=block, slots=slot...  11.3 us
  transfers between devices with their start and end apart: 22, of which 9 were waited for; matrix products, arithmetic and copies ran while one was open for 2% of the time, Pallas kernels for 16%

profile of v4, /device:TPU:0, one launch (start us, length us, event | category | flops | bytes accessed | tf_op | source)
XLA Modules:
  0.0 216.8 jit_solution(17153555333364568371)
XLA Ops:
  0.6 3.1 %prepare.2 = bf16[48,32,512]{2,1,0:T(8,128)(2,1)} custom-call(f32[16,32,4,8,128]{4,3,2,1,0:T(8,128)} %bitcast.13, f32[16,32,4,8,128]{4,3,2,1,0:T(8,128)} %bitcast.14, f32[16,32,4,8,128]{4,3,2,1,0:T(8,128)} %bitcast.15), custom_call_target="tpu_custom_call" | custom-call | flops 786432 | bytes 4718592 | tf_op jit(solution)/shard_map/prepare/pallas_call | solution.py:53
  3.7 7.4 %all-to-all-start = ((bf16[16,3,32,512]{3,2,1,0:T(8,128)(2,1)}), bf16[16,3,32,512]{3,2,1,0:T(8,128)(2,1)}, u32[]{:S(2)}, u32[]{:S(2)}) async-start(bf16[16,3,32,512]{3,2,1,0:T(8,128)(2,1)} %bitcast.2), calls=%async_computation | async-start | bytes 3145728 | tf_op jit(solution)/shard_map/all_to_all | solution.py:270
  11.1 4.1 %fusion.7 = (f32[512,512]{1,0:T(8,128)S(1)}, f32[512,512]{1,0:T(8,128)S(1)}) fusion(), kind=kLoop, calls=%fused_computation.16 | loop fusion | flops 3670016 | bytes 2097152 | tf_op jit(solution)/shard_map/sin | solution.py:31
  15.2 4.0 %prepare.3 = bf16[80,32,512]{2,1,0:T(8,128)(2,1)} custom-call(f32[16,32,4,8,128]{4,3,2,1,0:T(8,128)} %bitcast.16, f32[16,32,4,8,128]{4,3,2,1,0:T(8,128)} %bitcast.17, f32[16,32,4,8,128]{4,3,2,1,0:T(8,128)} %bitcast.18, f32[16,32,4,8,128]{4,3,2,1,0:T(8,128)} %bitcast.19, f32[16,32,4,8,128]{4,3,2,1,0:T(8,128)} %bitcast.20), custom_call_target="tpu_custom_call" | custom-call | flops 1310720 | bytes 7864320 | tf_op jit(solution)/shard_map/prepare/pallas_call | solution.py:53
  19.2 23.9 %all-to-all-done.x_ref = bf16[16,3,32,512]{3,2,1,0:T(8,128)(2,1)} async-done(((bf16[16,3,32,512]{3,2,1,0:T(8,128)(2,1)}), bf16[16,3,32,512]{3,2,1,0:T(8,128)(2,1)}, u32[]{:S(2)}, u32[]{:S(2)}) %all-to-all-start) | async-done | bytes 1572896 | tf_op jit(solution)/shard_map/all_to_all | solution.py:270
  43.2 9.2 %all-to-all-start.2 = ((bf16[16,5,32,512]{3,2,1,0:T(8,128)(2,1)}), bf16[16,5,32,512]{3,2,1,0:T(8,128)(2,1)}, u32[]{:S(2)}, u32[]{:S(2)}) async-start(bf16[16,5,32,512]{3,2,1,0:T(8,128)(2,1)} %bitcast.5), calls=%async_computation.2 | async-start | bytes 5242880 | tf_op jit(solution)/shard_map/all_to_all | solution.py:270
  52.3 1.2 copy-done.2
  53.5 6.9 %spectrum.2 = bf16[16,3,32,256]{3,2,1,0:T(8,128)(2,1)S(1)} custom-call(bf16[16,3,32,512]{3,2,1,0:T(8,128)(2,1)} %all-to-all-done.x_ref, bf16[1024,512]{1,0:T(8,128)(2,1)S(1)} %copy-done.2, f32[512,512]{1,0:T(8,128)S(1)} %get-tuple-element.16.cos_ref, f32[512,512]{1,0:T(8,128)S(1)} %get-tuple-element.17.sin_ref), custom_call_target="tpu_custom_call" | custom-call | flops 3221225472 | bytes 6553600 | tf_op jit(solution)/shard_map/spectrum/pallas_call | solution.py:95
  60.4 0.9 copy-done
  61.3 41.3 %all-to-all-done.2.x_ref = bf16[16,5,32,512]{3,2,1,0:T(8,128)(2,1)} async-done(((bf16[16,5,32,512]{3,2,1,0:T(8,128)(2,1)}), bf16[16,5,32,512]{3,2,1,0:T(8,128)(2,1)}, u32[]{:S(2)}, u32[]{:S(2)}) %all-to-all-start.2) | async-done | bytes 2621472 | tf_op jit(solution)/shard_map/all_to_all | solution.py:270
  102.6 13.3 %all-to-all-start.1 = ((bf16[16,3,32,256]{3,2,1,0:T(8,128)(2,1)}), bf16[16,3,32,256]{3,2,1,0:T(8,128)(2,1)S(1)}, u32[]{:S(2)}, u32[]{:S(2)}) async-start(bf16[16,3,32,256]{3,2,1,0:T(8,128)(2,1)} %copy-done), calls=%async_computation.1 | async-start | bytes 1572864 | tf_op jit(solution)/shard_map/all_to_all | solution.py:276
  116.0 1.2 copy-done.3
  117.2 11.4 %spectrum.3 = bf16[16,5,32,256]{3,2,1,0:T(8,128)(2,1)} custom-call(bf16[16,5,32,512]{3,2,1,0:T(8,128)(2,1)} %all-to-all-done.2.x_ref, bf16[1024,512]{1,0:T(8,128)(2,1)S(1)} %copy-done.3, f32[512,512]{1,0:T(8,128)S(1)} %get-tuple-element.16.cos_ref, f32[512,512]{1,0:T(8,128)S(1)} %get-tuple-element.17.sin_ref), custom_call_target="tpu_custom_call" | custom-call | flops 5368709120 | bytes 8126464 | tf_op jit(solution)/shard_map/spectrum/pallas_call | solution.py:95
  128.6 6.0 %all-to-all-done.1 = bf16[16,3,32,256]{3,2,1,0:T(8,128)(2,1)S(1)} async-done(((bf16[16,3,32,256]{3,2,1,0:T(8,128)(2,1)}), bf16[16,3,32,256]{3,2,1,0:T(8,128)(2,1)S(1)}, u32[]{:S(2)}, u32[]{:S(2)}) %all-to-all-start.1) | async-done | bytes 786464 | tf_op jit(solution)/shard_map/all_to_all | solution.py:276
  134.7 5.7 %all-to-all-start.3 = ((bf16[16,5,32,256]{3,2,1,0:T(8,128)(2,1)}), bf16[16,5,32,256]{3,2,1,0:T(8,128)(2,1)S(1)}, u32[]{:S(2)}, u32[]{:S(2)}) async-start(bf16[16,5,32,256]{3,2,1,0:T(8,128)(2,1)} %spectrum.3), calls=%async_computation.3 | async-start | bytes 2621440 | tf_op jit(solution)/shard_map/all_to_all | solution.py:276
  141.0 6.2 %product.2 = (f32[48,1024]{1,0:T(8,128)S(1)}, bf16[48,8192]{1,0:T(8,128)(2,1)S(1)}) custom-call(bf16[48,32,256]{2,1,0:T(8,128)(2,1)S(1)} %bitcast.12, bf16[8192,1024]{1,0:T(8,128)(2,1)} %weight_ref.3), custom_call_target="tpu_custom_call" | custom-call | flops 805306368 | bytes 16777216 | tf_op jit(solution)/shard_map/product/pallas_call | solution.py:195
  147.6 1.6 collective-permute-start.2
  149.5 18.0 %all-to-all-done.3 = bf16[16,5,32,256]{3,2,1,0:T(8,128)(2,1)S(1)} async-done(((bf16[16,5,32,256]{3,2,1,0:T(8,128)(2,1)}), bf16[16,5,32,256]{3,2,1,0:T(8,128)(2,1)S(1)}, u32[]{:S(2)}, u32[]{:S(2)}) %all-to-all-start.3) | async-done | bytes 1310752 | tf_op jit(solution)/shard_map/all_to_all | solution.py:276
  167.6 6.2 %product.3 = (f32[80,1024]{1,0:T(8,128)S(1)}, bf16[80,8192]{1,0:T(8,128)(2,1)S(1)}) custom-call(bf16[80,32,256]{2,1,0:T(8,128)(2,1)S(1)} %bitcast.11, bf16[8192,1024]{1,0:T(8,128)(2,1)} %weight_ref.3), custom_call_target="tpu_custom_call" | custom-call | flops 1342177280 | bytes 16777216 | tf_op jit(solution)/shard_map/product/pallas_call | solution.py:195
  174.7 2.0 collective-permute-start.11
  177.1 0.9 add_add_fusion.3
  178.0 4.5 %collective-permute-start.5 = (f32[48,256]{1,0:T(8,128)S(1)}, f32[48,256]{1,0:T(8,128)S(1)}, u32[]{:S(2)}, u32[]{:S(2)}) collective-permute-start(f32[48,256]{1,0:T(8,128)S(1)} %add_add_fusion.3), channel_id=1, source_target_pairs={{0,12},{1,13},{2,14},{3,15},{4,8},{5,9},{6,10},{7,11},{8,4},{9,5},... | collective-permute-start | bytes 147464 | tf_op jit(solution)/shard_map/ppermute | solution.py:157
  182.4 0.9 collective-permute-start.4
  183.9 3.0 %collective-permute-start.14 = (f32[80,256]{1,0:T(8,128)S(1)}, f32[80,256]{1,0:T(8,128)S(1)}, u32[]{:S(2)}, u32[]{:S(2)}) collective-permute-start(f32[80,256]{1,0:T(8,128)S(1)} %add_add_fusion.1), channel_id=1, source_target_pairs={{0,12},{1,13},{2,14},{3,15},{4,8},{5,9},{6,10},{7,11},{8,4},{9,5},... | collective-permute-start | bytes 245768 | tf_op jit(solution)/shard_map/ppermute | solution.py:157
  186.9 1.4 collective-permute-start.12
  188.5 2.7 %collective-permute-start.7 = (f32[48,256]{1,0:T(8,128)S(1)}, f32[48,256]{1,0:T(8,128)S(1)}, u32[]{:S(2)}, u32[]{:S(2)}) collective-permute-start(f32[48,256]{1,0:T(8,128)S(1)} %add_add_fusion.2), channel_id=1, source_target_pairs={{0,2},{1,3},{2,0},{3,1},{4,6},{5,7},{6,4},{7,5},{8,10},{9,11},{10,... | collective-permute-start | bytes 147464 | tf_op jit(solution)/shard_map/ppermute | solution.py:157
  191.2 3.7 %collective-permute-done.13 = f32[80,256]{1,0:T(8,128)S(1)} collective-permute-done((f32[80,256]{1,0:T(8,128)S(1)}, f32[80,256]{1,0:T(8,128)S(1)}, u32[]{:S(2)}, u32[]{:S(2)}) %collective-permute-start.13) | collective-permute-done | bytes 81952 | tf_op jit(solution)/shard_map/ppermute | solution.py:157
  195.1 1.4 collective-permute-start.16
  197.0 3.4 %collective-permute-done.16 = f32[80,256]{1,0:T(8,128)S(1)} collective-permute-done((f32[80,256]{1,0:T(8,128)S(1)}, f32[80,256]{1,0:T(8,128)S(1)}, u32[]{:S(2)}, u32[]{:S(2)}) %collective-permute-start.16) | collective-permute-done | bytes 81952 | tf_op jit(solution)/shard_map/ppermute | solution.py:157
  200.4 0.9 collective-permute-done.15
  202.8 1.6 convert_reduce_fusion
  204.4 11.3 %gradient.1 = f32[8192,1024]{1,0:T(8,128)} custom-call(bf16[48,8192]{1,0:T(8,128)(2,1)S(1)} %get-tuple-element.19.refs_0_, bf16[80,8192]{1,0:T(8,128)(2,1)S(1)} %get-tuple-element.20.refs_1_, bf16[128,1024]{1,0:T(8,128)(2,1)S(1)} %get-tuple-element.24.refs_2_), custom_call_target="tpu_custom_call" | custom-call | flops 2147483648 | bytes 33554432 | tf_op jit(solution)/shard_map/gradient/pallas_call | solution.py:137
  (45 shorter events, 4.0 us)
Async XLA Ops:
  3.7 39.5 %all-to-all-start = ((bf16[16,3,32,512]{3,2,1,0:T(8,128)(2,1)}), bf16[16,3,32,512]{3,2,1,0:T(8,128)(2,1)}, u32[]{:S(2)}, u32[]{:S(2)}) async-start(bf16[16,3,32,512]{3,2,1,0:T(8,128)(2,1)} %bitcast.2), calls=%async_computation | async-start | bytes 3145728 | tf_op jit(solution)/shard_map/all_to_all | solution.py:270
  43.2 59.5 %all-to-all-start.2 = ((bf16[16,5,32,512]{3,2,1,0:T(8,128)(2,1)}), bf16[16,5,32,512]{3,2,1,0:T(8,128)(2,1)}, u32[]{:S(2)}, u32[]{:S(2)}) async-start(bf16[16,5,32,512]{3,2,1,0:T(8,128)(2,1)} %bitcast.5), calls=%async_computation.2 | async-start | bytes 5242880 | tf_op jit(solution)/shard_map/all_to_all | solution.py:270
  52.3 1.2 copy-start.2
  60.4 0.9 copy-start
  102.6 32.0 %all-to-all-start.1 = ((bf16[16,3,32,256]{3,2,1,0:T(8,128)(2,1)}), bf16[16,3,32,256]{3,2,1,0:T(8,128)(2,1)S(1)}, u32[]{:S(2)}, u32[]{:S(2)}) async-start(bf16[16,3,32,256]{3,2,1,0:T(8,128)(2,1)} %copy-done), calls=%async_computation.1 | async-start | bytes 1572864 | tf_op jit(solution)/shard_map/all_to_all | solution.py:276
  115.9 1.2 copy-start.3
  134.7 32.9 %all-to-all-start.3 = ((bf16[16,5,32,256]{3,2,1,0:T(8,128)(2,1)}), bf16[16,5,32,256]{3,2,1,0:T(8,128)(2,1)S(1)}, u32[]{:S(2)}, u32[]{:S(2)}) async-start(bf16[16,5,32,256]{3,2,1,0:T(8,128)(2,1)} %spectrum.3), calls=%async_computation.3 | async-start | bytes 2621440 | tf_op jit(solution)/shard_map/all_to_all | solution.py:276
  147.3 20.3 %copy-start.1 = (f32[48,1024]{1,0:T(8,128)}, f32[48,1024]{1,0:T(8,128)S(1)}, u32[]{:S(2)}) copy-start(f32[48,1024]{1,0:T(8,128)S(1)} %get-tuple-element.13) | copy-start | bytes 589828
  147.3 29.4 %collective-permute-start = (f32[48,256]{1,0:T(8,128)S(1)}, f32[48,256]{1,0:T(8,128)}, u32[]{:S(2)}, u32[]{:S(2)}) collective-permute-start(f32[48,256]{1,0:T(8,128)S(1)} %get-tuple-element.39), channel_id=1, source_target_pairs={{0,1},{1,0},{2,3},{3,2},{4,5},{5,4},{6,7},{7,6},{8,9},{9,8},{10,11... | collective-permute-start | bytes 147464 | tf_op jit(solution)/shard_map/ppermute | solution.py:157
  147.6 29.5 %collective-permute-start.2 = (f32[48,256]{1,0:T(8,128)S(1)}, f32[48,256]{1,0:T(8,128)}, u32[]{:S(2)}, u32[]{:S(2)}) collective-permute-start(f32[48,256]{1,0:T(8,128)S(1)} %get-tuple-element.40), channel_id=1, source_target_pairs={{0,3},{1,2},{2,1},{3,0},{4,7},{5,6},{6,5},{7,4},{8,11},{9,10},{10,... | collective-permute-start | bytes 147464 | tf_op jit(solution)/shard_map/ppermute | solution.py:157
  149.2 27.9 %collective-permute-start.1 = (f32[48,256]{1,0:T(8,128)S(1)}, f32[48,256]{1,0:T(8,128)}, u32[]{:S(2)}, u32[]{:S(2)}) collective-permute-start(f32[48,256]{1,0:T(8,128)S(1)} %get-tuple-element.41), channel_id=1, source_target_pairs={{0,2},{1,3},{2,0},{3,1},{4,6},{5,7},{6,4},{7,5},{8,10},{9,11},{10,... | collective-permute-start | bytes 147464 | tf_op jit(solution)/shard_map/ppermute | solution.py:157
  173.8 27.5 %copy-start.4 = (f32[1024]{0:T(1024)S(1)}, f32[1024]{0:T(1024)}, u32[]{:S(2)}) copy-start(f32[1024]{0:T(1024)} %param.11) | copy-start | bytes 12292
  173.8 27.5 %copy-start.5 = (f32[1024]{0:T(1024)S(1)}, f32[1024]{0:T(1024)}, u32[]{:S(2)}) copy-start(f32[1024]{0:T(1024)} %param.10) | copy-start | bytes 12292
  173.8 27.7 %copy-start.6 = (s32[128]{0:T(128)S(1)}, s32[128]{0:T(128)}, u32[]{:S(2)}) copy-start(s32[128]{0:T(128)} %param.8) | copy-start | bytes 1540
  173.9 9.5 %collective-permute-start.9 = (f32[80,256]{1,0:T(8,128)S(1)}, f32[80,256]{1,0:T(8,128)S(1)}, u32[]{:S(2)}, u32[]{:S(2)}) collective-permute-start(f32[80,256]{1,0:T(8,128)S(1)} %get-tuple-element.32), channel_id=1, source_target_pairs={{0,1},{1,0},{2,3},{3,2},{4,5},{5,4},{6,7},{7,6},{8,9},{9,8},{10,11... | collective-permute-start | bytes 245768 | tf_op jit(solution)/shard_map/ppermute | solution.py:157
  174.7 9.1 %collective-permute-start.11 = (f32[80,256]{1,0:T(8,128)S(1)}, f32[80,256]{1,0:T(8,128)S(1)}, u32[]{:S(2)}, u32[]{:S(2)}) collective-permute-start(f32[80,256]{1,0:T(8,128)S(1)} %get-tuple-element.33), channel_id=1, source_target_pairs={{0,3},{1,2},{2,1},{3,0},{4,7},{5,6},{6,5},{7,4},{8,11},{9,10},{10,... | collective-permute-start | bytes 245768 | tf_op jit(solution)/shard_map/ppermute | solution.py:157
  176.7 7.1 %collective-permute-start.10 = (f32[80,256]{1,0:T(8,128)S(1)}, f32[80,256]{1,0:T(8,128)S(1)}, u32[]{:S(2)}, u32[]{:S(2)}) collective-permute-start(f32[80,256]{1,0:T(8,128)S(1)} %get-tuple-element.34), channel_id=1, source_target_pairs={{0,2},{1,3},{2,0},{3,1},{4,6},{5,7},{6,4},{7,5},{8,10},{9,11},{10,... | collective-permute-start | bytes 245768 | tf_op jit(solution)/shard_map/ppermute | solution.py:157
  178.0 9.0 %collective-permute-start.5 = (f32[48,256]{1,0:T(8,128)S(1)}, f32[48,256]{1,0:T(8,128)S(1)}, u32[]{:S(2)}, u32[]{:S(2)}) collective-permute-start(f32[48,256]{1,0:T(8,128)S(1)} %add_add_fusion.3), channel_id=1, source_target_pairs={{0,12},{1,13},{2,14},{3,15},{4,8},{5,9},{6,10},{7,11},{8,4},{9,5},... | collective-permute-start | bytes 147464 | tf_op jit(solution)/shard_map/ppermute | solution.py:157
  182.4 5.9 %collective-permute-start.4 = (f32[48,256]{1,0:T(8,128)S(1)}, f32[48,256]{1,0:T(8,128)S(1)}, u32[]{:S(2)}, u32[]{:S(2)}) collective-permute-start(f32[48,256]{1,0:T(8,128)S(1)} %add_add_fusion.3), channel_id=1, source_target_pairs={{0,8},{1,9},{2,10},{3,11},{4,12},{5,13},{6,14},{7,15},{8,0},{9,1},... | collective-permute-start | bytes 147464 | tf_op jit(solution)/shard_map/ppermute | solution.py:157
  183.3 5.1 %collective-permute-start.3 = (f32[48,256]{1,0:T(8,128)S(1)}, f32[48,256]{1,0:T(8,128)S(1)}, u32[]{:S(2)}, u32[]{:S(2)}) collective-permute-start(f32[48,256]{1,0:T(8,128)S(1)} %add_add_fusion.3), channel_id=1, source_target_pairs={{0,4},{1,5},{2,6},{3,7},{4,0},{5,1},{6,2},{7,3},{8,12},{9,13},{10,... | collective-permute-start | bytes 147464 | tf_op jit(solution)/shard_map/ppermute | solution.py:157
  183.9 7.4 %collective-permute-start.14 = (f32[80,256]{1,0:T(8,128)S(1)}, f32[80,256]{1,0:T(8,128)S(1)}, u32[]{:S(2)}, u32[]{:S(2)}) collective-permute-start(f32[80,256]{1,0:T(8,128)S(1)} %add_add_fusion.1), channel_id=1, source_target_pairs={{0,12},{1,13},{2,14},{3,15},{4,8},{5,9},{6,10},{7,11},{8,4},{9,5},... | collective-permute-start | bytes 245768 | tf_op jit(solution)/shard_map/ppermute | solution.py:157
  186.9 8.0 %collective-permute-start.13 = (f32[80,256]{1,0:T(8,128)S(1)}, f32[80,256]{1,0:T(8,128)S(1)}, u32[]{:S(2)}, u32[]{:S(2)}) collective-permute-start(f32[80,256]{1,0:T(8,128)S(1)} %add_add_fusion.1), channel_id=1, source_target_pairs={{0,8},{1,9},{2,10},{3,11},{4,12},{5,13},{6,14},{7,15},{8,0},{9,1},... | collective-permute-start | bytes 245768 | tf_op jit(solution)/shard_map/ppermute | solution.py:157
  186.9 8.0 %collective-permute-start.12 = (f32[80,256]{1,0:T(8,128)S(1)}, f32[80,256]{1,0:T(8,128)S(1)}, u32[]{:S(2)}, u32[]{:S(2)}) collective-permute-start(f32[80,256]{1,0:T(8,128)S(1)} %add_add_fusion.1), channel_id=1, source_target_pairs={{0,4},{1,5},{2,6},{3,7},{4,0},{5,1},{6,2},{7,3},{8,12},{9,13},{10,... | collective-permute-start | bytes 245768 | tf_op jit(solution)/shard_map/ppermute | solution.py:157
  188.4 8.1 %collective-permute-start.8 = (f32[48,256]{1,0:T(8,128)S(1)}, f32[48,256]{1,0:T(8,128)S(1)}, u32[]{:S(2)}, u32[]{:S(2)}) collective-permute-start(f32[48,256]{1,0:T(8,128)S(1)} %add_add_fusion.2), channel_id=1, source_target_pairs={{0,1},{1,0},{2,3},{3,2},{4,5},{5,4},{6,7},{7,6},{8,9},{9,8},{10,11... | collective-permute-start | bytes 147464 | tf_op jit(solution)/shard_map/ppermute | solution.py:157
  188.5 8.4 %collective-permute-start.7 = (f32[48,256]{1,0:T(8,128)S(1)}, f32[48,256]{1,0:T(8,128)S(1)}, u32[]{:S(2)}, u32[]{:S(2)}) collective-permute-start(f32[48,256]{1,0:T(8,128)S(1)} %add_add_fusion.2), channel_id=1, source_target_pairs={{0,2},{1,3},{2,0},{3,1},{4,6},{5,7},{6,4},{7,5},{8,10},{9,11},{10,... | collective-permute-start | bytes 147464 | tf_op jit(solution)/shard_map/ppermute | solution.py:157
  191.2 5.7 %collective-permute-start.6 = (f32[48,256]{1,0:T(8,128)S(1)}, f32[48,256]{1,0:T(8,128)S(1)}, u32[]{:S(2)}, u32[]{:S(2)}) collective-permute-start(f32[48,256]{1,0:T(8,128)S(1)} %add_add_fusion.2), channel_id=1, source_target_pairs={{0,3},{1,2},{2,1},{3,0},{4,7},{5,6},{6,5},{7,4},{8,11},{9,10},{10,... | collective-permute-start | bytes 147464 | tf_op jit(solution)/shard_map/ppermute | solution.py:157
  195.0 2.0 collective-permute-start.17
  195.1 5.3 %collective-permute-start.16 = (f32[80,256]{1,0:T(8,128)S(1)}, f32[80,256]{1,0:T(8,128)S(1)}, u32[]{:S(2)}, u32[]{:S(2)}) collective-permute-start(f32[80,256]{1,0:T(8,128)S(1)} %add_add_fusion), channel_id=1, source_target_pairs={{0,2},{1,3},{2,0},{3,1},{4,6},{5,7},{6,4},{7,5},{8,10},{9,11},{10,... | collective-permute-start | bytes 245768 | tf_op jit(solution)/shard_map/ppermute | solution.py:157
  196.5 4.7 %collective-permute-start.15 = (f32[80,256]{1,0:T(8,128)S(1)}, f32[80,256]{1,0:T(8,128)S(1)}, u32[]{:S(2)}, u32[]{:S(2)}) collective-permute-start(f32[80,256]{1,0:T(8,128)S(1)} %add_add_fusion), channel_id=1, source_target_pairs={{0,3},{1,2},{2,1},{3,0},{4,7},{5,6},{6,5},{7,4},{8,11},{9,10},{10,... | collective-permute-start | bytes 245768 | tf_op jit(solution)/shard_map/ppermute | solution.py:157

commit v5 on v4

--- a/solution.py
+++ b/solution.py
@@ -234,7 +234,9 @@
         while bit < devices:
             own = own + exchange(own, bit, devices)
             bit *= 2
+    own = lax.reduce_precision(own, 8, 7).astype(jnp.bfloat16)
     got = [own] + [exchange(own, k, devices) for k in range(1, 4)]
+    got = [part.astype(jnp.float32) for part in got]
     odd = (me % 2) == 1
     high = me >= 2
     low_pair = [jnp.where(odd, got[1], got[0]), jnp.where(odd, got[0], got[1])]

time: 217 us -> 216 us (level)
  no operation moved by 1% of the time
where the time goes in v5:
time: 216 us; the launch traced here: 215 us
  waiting for transfers between devices  96.3 us (45%)
  starting transfers between devices  55.9 us (26%)
  Pallas kernels  49.1 us (23%)
  other arithmetic  6.85 us (3%)
  local copies, waits for them, and re-layouts  3.4 us (2%)
  between operations  3.34 us (2%)
    all_to_all x2, waiting for transfers between devices, on_device(): blocks = lax.all_to_all(mine, 'tm', split_axis=0, concat_axis=0, tiled=True)  65.2 us
    all_to_all x2, waiting for transfers between devices, on_device(): feats = lax.all_to_all(feats, 'tm', split_axis=0, concat_axis=0, tiled=True)  24.1 us
    ppermute x18, starting transfers between devices, exchange(): return lax.ppermute(value, 'tm', [(i, i ^ bit) for i in range(devices)])  20.3 us
    all_to_all x2, starting transfers between devices, on_device(): feats = lax.all_to_all(feats, 'tm', split_axis=0, concat_axis=0, tiled=True)  19 us
    pallas_call x2, Pallas kernels, spectrum(): pl.pallas_call(functools.partial(spectrum_kernel, block=max(128, slow)),...  18.3 us
    all_to_all x2, starting transfers between devices, on_device(): blocks = lax.all_to_all(mine, 'tm', split_axis=0, concat_axis=0, tiled=True)  16.6 us
    pallas_call x2, Pallas kernels, product(): pl.pallas_call(functools.partial(product_kernel, step=step), in_specs=[vm...  12.5 us
    pallas_call x1, Pallas kernels, gradient(): pl.pallas_call(functools.partial(gradient_kernel, block=block, slots=slot...  11.3 us
  transfers between devices with their start and end apart: 22, of which 9 were waited for; matrix products, arithmetic and copies ran while one was open for 2% of the time, Pallas kernels for 16%

profile of v5, /device:TPU:0, one launch (start us, length us, event | category | flops | bytes accessed | tf_op | source)
XLA Modules:
  0.0 214.9 jit_solution(17402501204066773286)
XLA Ops:
  0.6 3.1 %prepare.2 = bf16[48,32,512]{2,1,0:T(8,128)(2,1)} custom-call(f32[16,32,4,8,128]{4,3,2,1,0:T(8,128)} %bitcast.13, f32[16,32,4,8,128]{4,3,2,1,0:T(8,128)} %bitcast.14, f32[16,32,4,8,128]{4,3,2,1,0:T(8,128)} %bitcast.15), custom_call_target="tpu_custom_call" | custom-call | flops 786432 | bytes 4718592 | tf_op jit(solution)/shard_map/prepare/pallas_call | solution.py:53
  3.7 7.4 %all-to-all-start = ((bf16[16,3,32,512]{3,2,1,0:T(8,128)(2,1)}), bf16[16,3,32,512]{3,2,1,0:T(8,128)(2,1)}, u32[]{:S(2)}, u32[]{:S(2)}) async-start(bf16[16,3,32,512]{3,2,1,0:T(8,128)(2,1)} %bitcast.2), calls=%async_computation | async-start | bytes 3145728 | tf_op jit(solution)/shard_map/all_to_all | solution.py:272
  11.1 4.1 %fusion.7 = (f32[512,512]{1,0:T(8,128)S(1)}, f32[512,512]{1,0:T(8,128)S(1)}) fusion(), kind=kLoop, calls=%fused_computation.16 | loop fusion | flops 3670016 | bytes 2097152 | tf_op jit(solution)/shard_map/sin | solution.py:31
  15.2 4.0 %prepare.3 = bf16[80,32,512]{2,1,0:T(8,128)(2,1)} custom-call(f32[16,32,4,8,128]{4,3,2,1,0:T(8,128)} %bitcast.16, f32[16,32,4,8,128]{4,3,2,1,0:T(8,128)} %bitcast.17, f32[16,32,4,8,128]{4,3,2,1,0:T(8,128)} %bitcast.18, f32[16,32,4,8,128]{4,3,2,1,0:T(8,128)} %bitcast.19, f32[16,32,4,8,128]{4,3,2,1,0:T(8,128)} %bitcast.20), custom_call_target="tpu_custom_call" | custom-call | flops 1310720 | bytes 7864320 | tf_op jit(solution)/shard_map/prepare/pallas_call | solution.py:53
  19.2 23.9 %all-to-all-done.x_ref = bf16[16,3,32,512]{3,2,1,0:T(8,128)(2,1)} async-done(((bf16[16,3,32,512]{3,2,1,0:T(8,128)(2,1)}), bf16[16,3,32,512]{3,2,1,0:T(8,128)(2,1)}, u32[]{:S(2)}, u32[]{:S(2)}) %all-to-all-start) | async-done | bytes 1572896 | tf_op jit(solution)/shard_map/all_to_all | solution.py:272
  43.2 9.2 %all-to-all-start.2 = ((bf16[16,5,32,512]{3,2,1,0:T(8,128)(2,1)}), bf16[16,5,32,512]{3,2,1,0:T(8,128)(2,1)}, u32[]{:S(2)}, u32[]{:S(2)}) async-start(bf16[16,5,32,512]{3,2,1,0:T(8,128)(2,1)} %bitcast.5), calls=%async_computation.2 | async-start | bytes 5242880 | tf_op jit(solution)/shard_map/all_to_all | solution.py:272
  52.3 1.2 copy-done.2
  53.6 6.9 %spectrum.2 = bf16[16,3,32,256]{3,2,1,0:T(8,128)(2,1)S(1)} custom-call(bf16[16,3,32,512]{3,2,1,0:T(8,128)(2,1)} %all-to-all-done.x_ref, bf16[1024,512]{1,0:T(8,128)(2,1)S(1)} %copy-done.2, f32[512,512]{1,0:T(8,128)S(1)} %get-tuple-element.16.cos_ref, f32[512,512]{1,0:T(8,128)S(1)} %get-tuple-element.17.sin_ref), custom_call_target="tpu_custom_call" | custom-call | flops 3221225472 | bytes 6553600 | tf_op jit(solution)/shard_map/spectrum/pallas_call | solution.py:95
  60.5 0.9 copy-done
  61.3 41.3 %all-to-all-done.2.x_ref = bf16[16,5,32,512]{3,2,1,0:T(8,128)(2,1)} async-done(((bf16[16,5,32,512]{3,2,1,0:T(8,128)(2,1)}), bf16[16,5,32,512]{3,2,1,0:T(8,128)(2,1)}, u32[]{:S(2)}, u32[]{:S(2)}) %all-to-all-start.2) | async-done | bytes 2621472 | tf_op jit(solution)/shard_map/all_to_all | solution.py:272
  102.6 13.3 %all-to-all-start.1 = ((bf16[16,3,32,256]{3,2,1,0:T(8,128)(2,1)}), bf16[16,3,32,256]{3,2,1,0:T(8,128)(2,1)S(1)}, u32[]{:S(2)}, u32[]{:S(2)}) async-start(bf16[16,3,32,256]{3,2,1,0:T(8,128)(2,1)} %copy-done), calls=%async_computation.1 | async-start | bytes 1572864 | tf_op jit(solution)/shard_map/all_to_all | solution.py:278
  116.0 1.2 copy-done.3
  117.2 11.4 %spectrum.3 = bf16[16,5,32,256]{3,2,1,0:T(8,128)(2,1)} custom-call(bf16[16,5,32,512]{3,2,1,0:T(8,128)(2,1)} %all-to-all-done.2.x_ref, bf16[1024,512]{1,0:T(8,128)(2,1)S(1)} %copy-done.3, f32[512,512]{1,0:T(8,128)S(1)} %get-tuple-element.16.cos_ref, f32[512,512]{1,0:T(8,128)S(1)} %get-tuple-element.17.sin_ref), custom_call_target="tpu_custom_call" | custom-call | flops 5368709120 | bytes 8126464 | tf_op jit(solution)/shard_map/spectrum/pallas_call | solution.py:95
  128.6 6.0 %all-to-all-done.1 = bf16[16,3,32,256]{3,2,1,0:T(8,128)(2,1)S(1)} async-done(((bf16[16,3,32,256]{3,2,1,0:T(8,128)(2,1)}), bf16[16,3,32,256]{3,2,1,0:T(8,128)(2,1)S(1)}, u32[]{:S(2)}, u32[]{:S(2)}) %all-to-all-start.1) | async-done | bytes 786464 | tf_op jit(solution)/shard_map/all_to_all | solution.py:278
  134.7 5.7 %all-to-all-start.3 = ((bf16[16,5,32,256]{3,2,1,0:T(8,128)(2,1)}), bf16[16,5,32,256]{3,2,1,0:T(8,128)(2,1)S(1)}, u32[]{:S(2)}, u32[]{:S(2)}) async-start(bf16[16,5,32,256]{3,2,1,0:T(8,128)(2,1)} %spectrum.3), calls=%async_computation.3 | async-start | bytes 2621440 | tf_op jit(solution)/shard_map/all_to_all | solution.py:278
  141.0 6.2 %product.2 = (f32[48,1024]{1,0:T(8,128)S(1)}, bf16[48,8192]{1,0:T(8,128)(2,1)S(1)}) custom-call(bf16[48,32,256]{2,1,0:T(8,128)(2,1)S(1)} %bitcast.12, bf16[8192,1024]{1,0:T(8,128)(2,1)} %weight_ref.3), custom_call_target="tpu_custom_call" | custom-call | flops 805306368 | bytes 16777216 | tf_op jit(solution)/shard_map/product/pallas_call | solution.py:195
  147.6 1.6 collective-permute-start.2
  149.5 18.0 %all-to-all-done.3 = bf16[16,5,32,256]{3,2,1,0:T(8,128)(2,1)S(1)} async-done(((bf16[16,5,32,256]{3,2,1,0:T(8,128)(2,1)}), bf16[16,5,32,256]{3,2,1,0:T(8,128)(2,1)S(1)}, u32[]{:S(2)}, u32[]{:S(2)}) %all-to-all-start.3) | async-done | bytes 1310752 | tf_op jit(solution)/shard_map/all_to_all | solution.py:278
  167.6 6.3 %product.3 = (f32[80,1024]{1,0:T(8,128)S(1)}, bf16[80,8192]{1,0:T(8,128)(2,1)S(1)}) custom-call(bf16[80,32,256]{2,1,0:T(8,128)(2,1)S(1)} %bitcast.11, bf16[8192,1024]{1,0:T(8,128)(2,1)} %weight_ref.3), custom_call_target="tpu_custom_call" | custom-call | flops 1342177280 | bytes 16777216 | tf_op jit(solution)/shard_map/product/pallas_call | solution.py:195
  174.7 2.0 collective-permute-start.11
  177.1 0.9 add_add_fusion.1
  178.0 4.5 %collective-permute-start.5 = (f32[48,256]{1,0:T(8,128)S(1)}, f32[48,256]{1,0:T(8,128)S(1)}, u32[]{:S(2)}, u32[]{:S(2)}) collective-permute-start(f32[48,256]{1,0:T(8,128)S(1)} %add_add_fusion.1), channel_id=1, source_target_pairs={{0,12},{1,13},{2,14},{3,15},{4,8},{5,9},{6,10},{7,11},{8,4},{9,5},... | collective-permute-start | bytes 147464 | tf_op jit(solution)/shard_map/ppermute | solution.py:157
  182.4 0.9 collective-permute-start.4
  183.9 3.0 %collective-permute-start.14 = (f32[80,256]{1,0:T(8,128)S(1)}, f32[80,256]{1,0:T(8,128)S(1)}, u32[]{:S(2)}, u32[]{:S(2)}) collective-permute-start(f32[80,256]{1,0:T(8,128)S(1)} %add_add_fusion), channel_id=1, source_target_pairs={{0,12},{1,13},{2,14},{3,15},{4,8},{5,9},{6,10},{7,11},{8,4},{9,5},... | collective-permute-start | bytes 245768 | tf_op jit(solution)/shard_map/ppermute | solution.py:157
  187.0 1.4 collective-permute-start.12
  188.5 2.6 %collective-permute-start.7 = (bf16[48,256]{1,0:T(8,128)(2,1)S(1)}, bf16[48,256]{1,0:T(8,128)(2,1)S(1)}, u32[]{:S(2)}, u32[]{:S(2)}) collective-permute-start(bf16[48,256]{1,0:T(8,128)(2,1)S(1)} %reduce-precision_convert_fusion.1), channel_id=1, source_target_pairs={{0,2},{1,3},{2,0},{3,1},{4,6},{5,7},{6,4},{7,5},{8,10},{9,11},{10,... | collective-permute-start | bytes 73736 | tf_op jit(solution)/shard_map/ppermute | solution.py:157
  191.3 3.7 %collective-permute-done.13 = f32[80,256]{1,0:T(8,128)S(1)} collective-permute-done((f32[80,256]{1,0:T(8,128)S(1)}, f32[80,256]{1,0:T(8,128)S(1)}, u32[]{:S(2)}, u32[]{:S(2)}) %collective-permute-start.13) | collective-permute-done | bytes 81952 | tf_op jit(solution)/shard_map/ppermute | solution.py:157
  195.1 1.4 collective-permute-start.16
  197.0 2.2 %collective-permute-done.16 = bf16[80,256]{1,0:T(8,128)(2,1)S(1)} collective-permute-done((bf16[80,256]{1,0:T(8,128)(2,1)S(1)}, bf16[80,256]{1,0:T(8,128)(2,1)S(1)}, u32[]{:S(2)}, u32[]{:S(2)}) %collective-permute-start.16) | collective-permute-done | bytes 40992 | tf_op jit(solution)/shard_map/ppermute | solution.py:157
  199.2 0.9 collective-permute-done.15
  201.6 0.9 convert_reduce_fusion
  202.5 11.3 %gradient.1 = f32[8192,1024]{1,0:T(8,128)} custom-call(bf16[48,8192]{1,0:T(8,128)(2,1)S(1)} %get-tuple-element.19.refs_0_, bf16[80,8192]{1,0:T(8,128)(2,1)S(1)} %get-tuple-element.20.refs_1_, bf16[128,1024]{1,0:T(8,128)(2,1)S(1)} %get-tuple-element.24.refs_2_), custom_call_target="tpu_custom_call" | custom-call | flops 2147483648 | bytes 33554432 | tf_op jit(solution)/shard_map/gradient/pallas_call | solution.py:137
  (47 shorter events, 4.1 us)
Async XLA Ops:
  3.7 39.5 %all-to-all-start = ((bf16[16,3,32,512]{3,2,1,0:T(8,128)(2,1)}), bf16[16,3,32,512]{3,2,1,0:T(8,128)(2,1)}, u32[]{:S(2)}, u32[]{:S(2)}) async-start(bf16[16,3,32,512]{3,2,1,0:T(8,128)(2,1)} %bitcast.2), calls=%async_computation | async-start | bytes 3145728 | tf_op jit(solution)/shard_map/all_to_all | solution.py:272
  43.2 59.5 %all-to-all-start.2 = ((bf16[16,5,32,512]{3,2,1,0:T(8,128)(2,1)}), bf16[16,5,32,512]{3,2,1,0:T(8,128)(2,1)}, u32[]{:S(2)}, u32[]{:S(2)}) async-start(bf16[16,5,32,512]{3,2,1,0:T(8,128)(2,1)} %bitcast.5), calls=%async_computation.2 | async-start | bytes 5242880 | tf_op jit(solution)/shard_map/all_to_all | solution.py:272
  52.3 1.2 copy-start.2
  60.4 0.9 copy-start
  102.6 32.0 %all-to-all-start.1 = ((bf16[16,3,32,256]{3,2,1,0:T(8,128)(2,1)}), bf16[16,3,32,256]{3,2,1,0:T(8,128)(2,1)S(1)}, u32[]{:S(2)}, u32[]{:S(2)}) async-start(bf16[16,3,32,256]{3,2,1,0:T(8,128)(2,1)} %copy-done), calls=%async_computation.1 | async-start | bytes 1572864 | tf_op jit(solution)/shard_map/all_to_all | solution.py:278
  116.0 1.2 copy-start.3
  134.7 32.9 %all-to-all-start.3 = ((bf16[16,5,32,256]{3,2,1,0:T(8,128)(2,1)}), bf16[16,5,32,256]{3,2,1,0:T(8,128)(2,1)S(1)}, u32[]{:S(2)}, u32[]{:S(2)}) async-start(bf16[16,5,32,256]{3,2,1,0:T(8,128)(2,1)} %spectrum.3), calls=%async_computation.3 | async-start | bytes 2621440 | tf_op jit(solution)/shard_map/all_to_all | solution.py:278
  147.3 20.3 %copy-start.1 = (f32[48,1024]{1,0:T(8,128)}, f32[48,1024]{1,0:T(8,128)S(1)}, u32[]{:S(2)}) copy-start(f32[48,1024]{1,0:T(8,128)S(1)} %get-tuple-element.13) | copy-start | bytes 589828
  147.3 29.4 %collective-permute-start = (f32[48,256]{1,0:T(8,128)S(1)}, f32[48,256]{1,0:T(8,128)}, u32[]{:S(2)}, u32[]{:S(2)}) collective-permute-start(f32[48,256]{1,0:T(8,128)S(1)} %get-tuple-element.31), channel_id=1, source_target_pairs={{0,1},{1,0},{2,3},{3,2},{4,5},{5,4},{6,7},{7,6},{8,9},{9,8},{10,11... | collective-permute-start | bytes 147464 | tf_op jit(solution)/shard_map/ppermute | solution.py:157
  147.6 29.5 %collective-permute-start.2 = (f32[48,256]{1,0:T(8,128)S(1)}, f32[48,256]{1,0:T(8,128)}, u32[]{:S(2)}, u32[]{:S(2)}) collective-permute-start(f32[48,256]{1,0:T(8,128)S(1)} %get-tuple-element.32), channel_id=1, source_target_pairs={{0,3},{1,2},{2,1},{3,0},{4,7},{5,6},{6,5},{7,4},{8,11},{9,10},{10,... | collective-permute-start | bytes 147464 | tf_op jit(solution)/shard_map/ppermute | solution.py:157
  149.2 27.9 %collective-permute-start.1 = (f32[48,256]{1,0:T(8,128)S(1)}, f32[48,256]{1,0:T(8,128)}, u32[]{:S(2)}, u32[]{:S(2)}) collective-permute-start(f32[48,256]{1,0:T(8,128)S(1)} %get-tuple-element.33), channel_id=1, source_target_pairs={{0,2},{1,3},{2,0},{3,1},{4,6},{5,7},{6,4},{7,5},{8,10},{9,11},{10,... | collective-permute-start | bytes 147464 | tf_op jit(solution)/shard_map/ppermute | solution.py:157
  167.6 32.5 %copy-start.4 = (f32[1024]{0:T(1024)S(1)}, f32[1024]{0:T(1024)}, u32[]{:S(2)}) copy-start(f32[1024]{0:T(1024)} %param.11) | copy-start | bytes 12292
  167.6 32.5 %copy-start.6 = (f32[1024]{0:T(1024)S(1)}, f32[1024]{0:T(1024)}, u32[]{:S(2)}) copy-start(f32[1024]{0:T(1024)} %param.10) | copy-start | bytes 12292
  173.8 26.5 %copy-start.7 = (s32[128]{0:T(128)S(1)}, s32[128]{0:T(128)}, u32[]{:S(2)}) copy-start(s32[128]{0:T(128)} %param.8) | copy-start | bytes 1540
  173.9 27.8 %copy-start.5 = (f32[1024]{0:T(1024)S(1)}, f32[1024]{0:T(1024)}, u32[]{:S(2)}) copy-start(f32[1024]{0:T(1024)} %param.11) | copy-start | bytes 12292
  173.9 9.5 %collective-permute-start.9 = (f32[80,256]{1,0:T(8,128)S(1)}, f32[80,256]{1,0:T(8,128)S(1)}, u32[]{:S(2)}, u32[]{:S(2)}) collective-permute-start(f32[80,256]{1,0:T(8,128)S(1)} %get-tuple-element.28), channel_id=1, source_target_pairs={{0,1},{1,0},{2,3},{3,2},{4,5},{5,4},{6,7},{7,6},{8,9},{9,8},{10,11... | collective-permute-start | bytes 245768 | tf_op jit(solution)/shard_map/ppermute | solution.py:157
  174.7 9.1 %collective-permute-start.11 = (f32[80,256]{1,0:T(8,128)S(1)}, f32[80,256]{1,0:T(8,128)S(1)}, u32[]{:S(2)}, u32[]{:S(2)}) collective-permute-start(f32[80,256]{1,0:T(8,128)S(1)} %get-tuple-element.29), channel_id=1, source_target_pairs={{0,3},{1,2},{2,1},{3,0},{4,7},{5,6},{6,5},{7,4},{8,11},{9,10},{10,... | collective-permute-start | bytes 245768 | tf_op jit(solution)/shard_map/ppermute | solution.py:157
  176.7 7.1 %collective-permute-start.10 = (f32[80,256]{1,0:T(8,128)S(1)}, f32[80,256]{1,0:T(8,128)S(1)}, u32[]{:S(2)}, u32[]{:S(2)}) collective-permute-start(f32[80,256]{1,0:T(8,128)S(1)} %get-tuple-element.30), channel_id=1, source_target_pairs={{0,2},{1,3},{2,0},{3,1},{4,6},{5,7},{6,4},{7,5},{8,10},{9,11},{10,... | collective-permute-start | bytes 245768 | tf_op jit(solution)/shard_map/ppermute | solution.py:157
  178.0 9.0 %collective-permute-start.5 = (f32[48,256]{1,0:T(8,128)S(1)}, f32[48,256]{1,0:T(8,128)S(1)}, u32[]{:S(2)}, u32[]{:S(2)}) collective-permute-start(f32[48,256]{1,0:T(8,128)S(1)} %add_add_fusion.1), channel_id=1, source_target_pairs={{0,12},{1,13},{2,14},{3,15},{4,8},{5,9},{6,10},{7,11},{8,4},{9,5},... | collective-permute-start | bytes 147464 | tf_op jit(solution)/shard_map/ppermute | solution.py:157
  182.4 5.9 %collective-permute-start.4 = (f32[48,256]{1,0:T(8,128)S(1)}, f32[48,256]{1,0:T(8,128)S(1)}, u32[]{:S(2)}, u32[]{:S(2)}) collective-permute-start(f32[48,256]{1,0:T(8,128)S(1)} %add_add_fusion.1), channel_id=1, source_target_pairs={{0,8},{1,9},{2,10},{3,11},{4,12},{5,13},{6,14},{7,15},{8,0},{9,1},... | collective-permute-start | bytes 147464 | tf_op jit(solution)/shard_map/ppermute | solution.py:157
  183.4 5.1 %collective-permute-start.3 = (f32[48,256]{1,0:T(8,128)S(1)}, f32[48,256]{1,0:T(8,128)S(1)}, u32[]{:S(2)}, u32[]{:S(2)}) collective-permute-start(f32[48,256]{1,0:T(8,128)S(1)} %add_add_fusion.1), channel_id=1, source_target_pairs={{0,4},{1,5},{2,6},{3,7},{4,0},{5,1},{6,2},{7,3},{8,12},{9,13},{10,... | collective-permute-start | bytes 147464 | tf_op jit(solution)/shard_map/ppermute | solution.py:157
  183.9 7.4 %collective-permute-start.14 = (f32[80,256]{1,0:T(8,128)S(1)}, f32[80,256]{1,0:T(8,128)S(1)}, u32[]{:S(2)}, u32[]{:S(2)}) collective-permute-start(f32[80,256]{1,0:T(8,128)S(1)} %add_add_fusion), channel_id=1, source_target_pairs={{0,12},{1,13},{2,14},{3,15},{4,8},{5,9},{6,10},{7,11},{8,4},{9,5},... | collective-permute-start | bytes 245768 | tf_op jit(solution)/shard_map/ppermute | solution.py:157
  186.9 8.0 %collective-permute-start.13 = (f32[80,256]{1,0:T(8,128)S(1)}, f32[80,256]{1,0:T(8,128)S(1)}, u32[]{:S(2)}, u32[]{:S(2)}) collective-permute-start(f32[80,256]{1,0:T(8,128)S(1)} %add_add_fusion), channel_id=1, source_target_pairs={{0,8},{1,9},{2,10},{3,11},{4,12},{5,13},{6,14},{7,15},{8,0},{9,1},... | collective-permute-start | bytes 245768 | tf_op jit(solution)/shard_map/ppermute | solution.py:157
  187.0 8.0 %collective-permute-start.12 = (f32[80,256]{1,0:T(8,128)S(1)}, f32[80,256]{1,0:T(8,128)S(1)}, u32[]{:S(2)}, u32[]{:S(2)}) collective-permute-start(f32[80,256]{1,0:T(8,128)S(1)} %add_add_fusion), channel_id=1, source_target_pairs={{0,4},{1,5},{2,6},{3,7},{4,0},{5,1},{6,2},{7,3},{8,12},{9,13},{10,... | collective-permute-start | bytes 245768 | tf_op jit(solution)/shard_map/ppermute | solution.py:157
  188.4 8.1 %collective-permute-start.8 = (bf16[48,256]{1,0:T(8,128)(2,1)S(1)}, bf16[48,256]{1,0:T(8,128)(2,1)S(1)}, u32[]{:S(2)}, u32[]{:S(2)}) collective-permute-start(bf16[48,256]{1,0:T(8,128)(2,1)S(1)} %reduce-precision_convert_fusion.1), channel_id=1, source_target_pairs={{0,1},{1,0},{2,3},{3,2},{4,5},{5,4},{6,7},{7,6},{8,9},{9,8},{10,11... | collective-permute-start | bytes 73736 | tf_op jit(solution)/shard_map/ppermute | solution.py:157
  188.5 8.4 %collective-permute-start.7 = (bf16[48,256]{1,0:T(8,128)(2,1)S(1)}, bf16[48,256]{1,0:T(8,128)(2,1)S(1)}, u32[]{:S(2)}, u32[]{:S(2)}) collective-permute-start(bf16[48,256]{1,0:T(8,128)(2,1)S(1)} %reduce-precision_convert_fusion.1), channel_id=1, source_target_pairs={{0,2},{1,3},{2,0},{3,1},{4,6},{5,7},{6,4},{7,5},{8,10},{9,11},{10,... | collective-permute-start | bytes 73736 | tf_op jit(solution)/shard_map/ppermute | solution.py:157
  191.2 5.7 %collective-permute-start.6 = (bf16[48,256]{1,0:T(8,128)(2,1)S(1)}, bf16[48,256]{1,0:T(8,128)(2,1)S(1)}, u32[]{:S(2)}, u32[]{:S(2)}) collective-permute-start(bf16[48,256]{1,0:T(8,128)(2,1)S(1)} %reduce-precision_convert_fusion.1), channel_id=1, source_target_pairs={{0,3},{1,2},{2,1},{3,0},{4,7},{5,6},{6,5},{7,4},{8,11},{9,10},{10,... | collective-permute-start | bytes 73736 | tf_op jit(solution)/shard_map/ppermute | solution.py:157
  195.0 2.0 collective-permute-start.17
  195.1 4.1 %collective-permute-start.16 = (bf16[80,256]{1,0:T(8,128)(2,1)S(1)}, bf16[80,256]{1,0:T(8,128)(2,1)S(1)}, u32[]{:S(2)}, u32[]{:S(2)}) collective-permute-start(bf16[80,256]{1,0:T(8,128)(2,1)S(1)} %reduce-precision_convert_fusion), channel_id=1, source_target_pairs={{0,2},{1,3},{2,0},{3,1},{4,6},{5,7},{6,4},{7,5},{8,10},{9,11},{10,... | collective-permute-start | bytes 122888 | tf_op jit(solution)/shard_map/ppermute | solution.py:157
  196.5 3.5 %collective-permute-start.15 = (bf16[80,256]{1,0:T(8,128)(2,1)S(1)}, bf16[80,256]{1,0:T(8,128)(2,1)S(1)}, u32[]{:S(2)}, u32[]{:S(2)}) collective-permute-start(bf16[80,256]{1,0:T(8,128)(2,1)S(1)} %reduce-precision_convert_fusion), channel_id=1, source_target_pairs={{0,3},{1,2},{2,1},{3,0},{4,7},{5,6},{6,5},{7,4},{8,11},{9,10},{10,... | collective-permute-start | bytes 122888 | tf_op jit(solution)/shard_map/ppermute | solution.py:157
